TPU v7x, 128 devices: a whole 4x4x4 slice. The times are simulated.
128 devices in a mesh: grp: 4 (over z_lo, core), dev: 32 (over x, y, z_hi).
Axes of the slice: x: 4, y: 4, z: 4 (z_hi: 2, z_lo: 2; z = z_hi * 2 + z_lo), core: 2. Of those that a mesh axis runs over, the one named last changes fastest.
Arguments:
- dosage: bfloat16 [2048, 131072], P('dev', 'grp'), may hold values from 0 to 2
- variant_slot: int32 [1024], replicated, may hold values from 0 to 2047, as said below
- center: float32 [1024], replicated, may hold values from 0.5 to 1.5
- variant_scale: float32 [1024], replicated, may hold values from 0.3 to 3
- sample_signs: int32 [131072], P(('grp', 'dev')), may hold values from -1 to 1, as said below
- sample_perm: int32 [131072], P(('grp', 'dev')), may hold values from 0 to 131071, as said below
- sample_rows: int32 [4096], P(('grp', 'dev')), may hold values from 0 to 131071, as said below
- projection: bfloat16 [1024, 256], replicated, may hold values from -0.1875 to 0.1875
Outputs:
- sketch: float32 [4096, 256], P(('grp', 'dev'))
Inputs may be any that keep to these rules, and one draw needn't show every extreme that they name: `variant_slot`: each slot holds at most one variant; file f holds its variants in its first slots; the last file, 31, is full with 64 variants; every other file holds at most 32. `sample_signs`: each value is -1 or +1. `sample_perm`: a permutation that maps each aligned block of 1024 positions onto the same block. `sample_rows`: rows m with the same m // 32 = b hold distinct positions of block b, between b * 1024 and (b + 1) * 1024 - 1.
All inputs are finite; a program needn't handle non-finite values.
Results may differ from a plain program's by a relative error of at most 0.0091.
Values may be sent and summed in bfloat16 or wider, within the bound.
No kernel may reach another device: no remote copies, remote signals or barrier semaphores. Data moves between devices by JAX's collectives and lax.ppermute only.
A program may use at most 64 MiB of HBM per device.

v0:
```python
import math

import jax
import jax.numpy as jnp
from jax import lax
from jax.sharding import PartitionSpec as P

root_half = 0.7071067811865476


def partner_2(shard, axis, distance):
    return lax.ppermute(shard, axis, [(i, i ^ 1 << distance) for i in range(lax.axis_size(axis))])


def hadamard_table(order):
    positions = jnp.arange(order, dtype=jnp.int32)
    common_bits = jnp.bitwise_and(positions[:, None], positions[None, :])
    parity = jnp.zeros((order, order), jnp.int32)
    for section_bit in range(order.bit_length() - 1):
        parity = parity + common_bits // 2**section_bit % 2
    return (1 - 2 * (parity % 2)).astype(jnp.bfloat16)


def pair_step(mine, partner, dev_index, section_bit):
    bit_value = dev_index // 2**section_bit % 2
    flip_sign = (1 - 2 * bit_value).astype(jnp.float32)
    return (
        (flip_sign * mine.astype(jnp.float32) + partner.astype(jnp.float32)) * root_half
    ).astype(jnp.bfloat16)


def on_device(
    dosage, variant_slot, center, variant_scale, sample_signs, sample_perm, sample_rows, projection
):
    slots_all = lax.all_to_all(dosage, "dev", split_axis=1, concat_axis=0, tiled=True)
    local_count = slots_all.shape[1]
    genotype = jnp.take(slots_all, variant_slot, axis=0)
    genotype = jnp.take(genotype, sample_perm % local_count, axis=1)
    signed = (
        (genotype.astype(jnp.float32) - center[:, None])
        * variant_scale[:, None]
        * sample_signs.astype(jnp.float32)[None, :]
    ).astype(jnp.bfloat16)
    projected = lax.dot_general(
        projection, signed, (((0,), (0,)), ((), ())), preferred_element_type=jnp.float32
    ).astype(jnp.bfloat16)
    local_mix = jnp.dot(projected, hadamard_table(local_count), preferred_element_type=jnp.float32)
    mixed_data = (local_mix * (1.0 / math.sqrt(local_count))).astype(jnp.bfloat16)
    dev_index = lax.axis_index("dev")
    for section_bit in range(lax.axis_size("dev").bit_length() - 1):
        partner = partner_2(mixed_data, "dev", section_bit)
        mixed_data = pair_step(mixed_data, partner, dev_index, section_bit)
    grp_index = lax.axis_index("grp")
    for section_bit in range(lax.axis_size("grp").bit_length() - 1):
        partner = partner_2(mixed_data, "grp", section_bit)
        mixed_data = pair_step(mixed_data, partner, grp_index, section_bit)
    block_start = (
        lax.axis_index("grp") * lax.axis_size("dev") + lax.axis_index("dev")
    ) * local_count
    local_rows = jnp.clip(sample_rows - block_start, 0, local_count - 1)
    columns = jnp.take(mixed_data, local_rows, axis=1)
    return jnp.transpose(columns).astype(jnp.float32)


def solution(mesh):
    return jax.shard_map(
        on_device,
        mesh=mesh,
        in_specs=(
            P("dev", "grp"),
            P(),
            P(),
            P(),
            P(("grp", "dev")),
            P(("grp", "dev")),
            P(("grp", "dev")),
            P(),
        ),
        out_specs=P(("grp", "dev"), None),
        check_vma=False,
    )
```

profile of v0, /device:TPU:1, one launch (start us, length us, event | category | flops | bytes accessed | tf_op | source)
XLA Modules:
  0.0 200.1 jit_solution(15658089677367092072)
XLA Ops:
  0.0 4.9 %copy.14 = bf16[8,32,8,1024]{3,2,0,1:T(8,128)(2,1)} copy(bf16[8,32,8,1024]{3,2,1,0:T(8,128)(2,1)} %bitcast.9) | data formatting | bytes 8388608 | tf_op jit(solution)/shard_map/all_to_all | solution.py:35
  4.9 11.4 %all-to-all-start = ((bf16[64,32,1024]{2,0,1:T(8,128)(2,1)}), bf16[64,32,1024]{2,0,1:T(8,128)(2,1)}, u32[]{:S(2)}, u32[]{:S(2)}) async-start(bf16[64,32,1024]{2,0,1:T(8,128)(2,1)} %bitcast.8), calls=%async_computation | async-start | bytes 8388608 | tf_op jit(solution)/shard_map/all_to_all | solution.py:35
  16.4 61.1 %all-to-all-done = bf16[64,32,1024]{2,0,1:T(8,128)(2,1)} async-done(((bf16[64,32,1024]{2,0,1:T(8,128)(2,1)}), bf16[64,32,1024]{2,0,1:T(8,128)(2,1)}, u32[]{:S(2)}, u32[]{:S(2)}) %all-to-all-start) | async-done | bytes 4194336 | tf_op jit(solution)/shard_map/all_to_all | solution.py:35
  77.6 7.7 %gather_fusion = bf16[1024,1024]{1,0:T(8,128)(2,1)S(1)} fusion(bf16[2048,1024]{1,0:T(8,128)(2,1)} %bitcast.1, s32[1024]{0:T(1024)S(1)} %fusion.76), kind=kCustom, calls=%fused_computation | custom fusion | bytes 4198400 | tf_op jit(solution)/shard_map/jit(_take)/gather | solution.py:37
  85.3 1.6 broadcast_select_fusion
  86.9 2.9 %copy.10 = bf16[1024,1024]{0,1:T(8,128)(2,1)S(1)} copy(bf16[1024,1024]{1,0:T(8,128)(2,1)} %broadcast_select_fusion) | data formatting | bytes 4194304 | tf_op jit(solution)/shard_map/jit(_take)/select_n | solution.py:37
  89.8 5.4 %gather_fusion.1 = bf16[1024,1024]{1,0:T(8,128)(2,1)} fusion(bf16[1024,1024]{0,1:T(8,128)(2,1)S(1)} %copy.10, s32[1024]{0:T(1024)S(1)} %broadcast_clamp_fusion), kind=kCustom, calls=%fused_computation.1 | custom fusion | bytes 4198400 | tf_op jit(solution)/shard_map/jit(_take)/gather | solution.py:38
  95.2 21.6 %fusion.71 = bf16[256,1024]{1,0:T(8,128)(2,1)S(1)} fusion(bf16[1024,256]{1,0:T(8,128)(2,1)S(1)} %copy-done, f32[1024]{0:T(1024)S(1)} %convert_element_type.117, f32[1024]{0:T(1024)S(1)} %copy-done.5, f32[1024]{0:T(1024)S(1)} %copy-done.6, bf16[1024,1024]{1,0:T(8,128)(2,1)} %gather_fusion.1, pred[1024]{0:T(1024)(128)(4,1)S(1)} %compare_and_fusion.1), kind=kOutput, calls=%fused_computation.135 | convolution fusion | flops 1313603584 | bytes 3159040 | tf_op jit(solution)/shard_map/dot_general | solution.py:47
  116.7 0.1 collective-permute-start
  116.8 13.9 %collective-permute-done = bf16[256,1024]{1,0:T(8,128)(2,1)S(1)} collective-permute-done((bf16[256,1024]{1,0:T(8,128)(2,1)S(1)}, bf16[256,1024]{1,0:T(8,128)(2,1)S(1)}, u32[]{:S(2)}, u32[]{:S(2)}) %collective-permute-start) | collective-permute-done | bytes 524320 | tf_op jit(solution)/shard_map/ppermute | solution.py:12
  130.8 0.2 multiply_convert_fusion.10
  131.0 0.1 collective-permute-start.1
  131.1 11.5 %collective-permute-done.1 = bf16[256,1024]{1,0:T(8,128)(2,1)S(1)} collective-permute-done((bf16[256,1024]{1,0:T(8,128)(2,1)S(1)}, bf16[256,1024]{1,0:T(8,128)(2,1)S(1)}, u32[]{:S(2)}, u32[]{:S(2)}) %collective-permute-start.1) | collective-permute-done | bytes 524320 | tf_op jit(solution)/shard_map/ppermute | solution.py:12
  142.6 0.2 multiply_convert_fusion.9
  142.9 0.1 collective-permute-start.2
  143.0 11.6 %collective-permute-done.2 = bf16[256,1024]{1,0:T(8,128)(2,1)S(1)} collective-permute-done((bf16[256,1024]{1,0:T(8,128)(2,1)S(1)}, bf16[256,1024]{1,0:T(8,128)(2,1)S(1)}, u32[]{:S(2)}, u32[]{:S(2)}) %collective-permute-start.2) | collective-permute-done | bytes 524320 | tf_op jit(solution)/shard_map/ppermute | solution.py:12
  154.6 0.2 multiply_convert_fusion.8
  154.9 0.1 collective-permute-start.3
  155.0 9.3 %collective-permute-done.3 = bf16[256,1024]{1,0:T(8,128)(2,1)S(1)} collective-permute-done((bf16[256,1024]{1,0:T(8,128)(2,1)S(1)}, bf16[256,1024]{1,0:T(8,128)(2,1)S(1)}, u32[]{:S(2)}, u32[]{:S(2)}) %collective-permute-start.3) | collective-permute-done | bytes 524320 | tf_op jit(solution)/shard_map/ppermute | solution.py:12
  164.3 0.2 multiply_convert_fusion.7
  164.5 0.1 collective-permute-start.4
  164.6 9.5 %collective-permute-done.4 = bf16[256,1024]{1,0:T(8,128)(2,1)S(1)} collective-permute-done((bf16[256,1024]{1,0:T(8,128)(2,1)S(1)}, bf16[256,1024]{1,0:T(8,128)(2,1)S(1)}, u32[]{:S(2)}, u32[]{:S(2)}) %collective-permute-start.4) | collective-permute-done | bytes 524320 | tf_op jit(solution)/shard_map/ppermute | solution.py:12
  174.1 0.2 multiply_convert_fusion.6
  174.4 9.0 %collective-permute-start.5 = (bf16[256,1024]{1,0:T(8,128)(2,1)S(1)}, bf16[256,1024]{1,0:T(8,128)(2,1)S(1)}, u32[]{:S(2)}, u32[]{:S(2)}) collective-permute-start(bf16[256,1024]{1,0:T(8,128)(2,1)S(1)} %multiply_convert_fusion.6), channel_id=1, source_target_pairs={{0,32},{32,0},{64,96},{96,64},{1,33},{33,1},{65,97},{97,65},{2,34}... | collective-permute-start | bytes 1572872 | tf_op jit(solution)/shard_map/ppermute | solution.py:12
  183.4 1.5 collective-permute-done.5
  184.9 0.2 multiply_convert_fusion.5
  185.1 0.8 collective-permute-start.6
  186.0 12.3 %collective-permute-done.6 = bf16[256,1024]{1,0:T(8,128)(2,1)S(1)} collective-permute-done((bf16[256,1024]{1,0:T(8,128)(2,1)S(1)}, bf16[256,1024]{1,0:T(8,128)(2,1)S(1)}, u32[]{:S(2)}, u32[]{:S(2)}) %collective-permute-start.6) | collective-permute-done | bytes 524320 | tf_op jit(solution)/shard_map/ppermute | solution.py:12
  198.3 0.2 multiply_convert_fusion.4
  198.5 0.2 copy.11
  198.8 0.6 gather_fusion.2
  199.4 0.7 select_convert_fusion
  (21 shorter events, 0.1 us)
Async XLA Ops:
  0.0 95.2 %copy-start = (bf16[1024,256]{1,0:T(8,128)(2,1)S(1)}, bf16[1024,256]{1,0:T(8,128)(2,1)}, u32[]{:S(2)}) copy-start(bf16[1024,256]{1,0:T(8,128)(2,1)} %param.15) | copy-start | bytes 1572868
  4.9 11.4 %copy-start.3 = (s32[1024]{0:T(1024)S(1)}, s32[1024]{0:T(1024)}, u32[]{:S(2)}) copy-start(s32[1024]{0:T(1024)} %param.12) | copy-start | bytes 12292
  4.9 11.5 %copy-start.1 = (s32[1024]{0:T(1024)S(1)}, s32[1024]{0:T(1024)}, u32[]{:S(2)}) copy-start(s32[1024]{0:T(1024)} %param.9) | copy-start | bytes 12292
  4.9 11.5 %copy-start.2 = (s32[1024]{0:T(1024)S(1)}, s32[1024]{0:T(1024)}, u32[]{:S(2)}) copy-start(s32[1024]{0:T(1024)} %param.13) | copy-start | bytes 12292
  4.9 72.7 %all-to-all-start = ((bf16[64,32,1024]{2,0,1:T(8,128)(2,1)}), bf16[64,32,1024]{2,0,1:T(8,128)(2,1)}, u32[]{:S(2)}, u32[]{:S(2)}) async-start(bf16[64,32,1024]{2,0,1:T(8,128)(2,1)} %bitcast.8), calls=%async_computation | async-start | bytes 8388608 | tf_op jit(solution)/shard_map/all_to_all | solution.py:35
  89.7 5.4 %copy-start.5 = (f32[1024]{0:T(1024)S(1)}, f32[1024]{0:T(1024)}, u32[]{:S(2)}) copy-start(f32[1024]{0:T(1024)} %param.11) | copy-start | bytes 12292
  89.7 5.4 %copy-start.6 = (f32[1024]{0:T(1024)S(1)}, f32[1024]{0:T(1024)}, u32[]{:S(2)}) copy-start(f32[1024]{0:T(1024)} %param.10) | copy-start | bytes 12292
  116.7 14.0 %collective-permute-start = (bf16[256,1024]{1,0:T(8,128)(2,1)S(1)}, bf16[256,1024]{1,0:T(8,128)(2,1)S(1)}, u32[]{:S(2)}, u32[]{:S(2)}) collective-permute-start(bf16[256,1024]{1,0:T(8,128)(2,1)S(1)} %fusion.71), channel_id=1, source_target_pairs={{0,1},{1,0},{2,3},{3,2},{4,5},{5,4},{6,7},{7,6},{8,9},{9,8},{10,11... | collective-permute-start | bytes 1572872 | tf_op jit(solution)/shard_map/ppermute | solution.py:12
  131.0 55.0 %copy-start.4 = (s32[32]{0:T(128)S(1)}, s32[32]{0:T(128)}, u32[]{:S(2)}) copy-start(s32[32]{0:T(128)} %param.14) | copy-start | bytes 388
  131.0 11.6 %collective-permute-start.1 = (bf16[256,1024]{1,0:T(8,128)(2,1)S(1)}, bf16[256,1024]{1,0:T(8,128)(2,1)S(1)}, u32[]{:S(2)}, u32[]{:S(2)}) collective-permute-start(bf16[256,1024]{1,0:T(8,128)(2,1)S(1)} %multiply_convert_fusion.10), channel_id=1, source_target_pairs={{0,2},{1,3},{2,0},{3,1},{4,6},{5,7},{6,4},{7,5},{8,10},{9,11},{10,... | collective-permute-start | bytes 1572872 | tf_op jit(solution)/shard_map/ppermute | solution.py:12
  142.9 11.8 %collective-permute-start.2 = (bf16[256,1024]{1,0:T(8,128)(2,1)S(1)}, bf16[256,1024]{1,0:T(8,128)(2,1)S(1)}, u32[]{:S(2)}, u32[]{:S(2)}) collective-permute-start(bf16[256,1024]{1,0:T(8,128)(2,1)S(1)} %multiply_convert_fusion.9), channel_id=1, source_target_pairs={{0,4},{1,5},{2,6},{3,7},{4,0},{5,1},{6,2},{7,3},{8,12},{9,13},{10,... | collective-permute-start | bytes 1572872 | tf_op jit(solution)/shard_map/ppermute | solution.py:12
  154.9 9.4 %collective-permute-start.3 = (bf16[256,1024]{1,0:T(8,128)(2,1)S(1)}, bf16[256,1024]{1,0:T(8,128)(2,1)S(1)}, u32[]{:S(2)}, u32[]{:S(2)}) collective-permute-start(bf16[256,1024]{1,0:T(8,128)(2,1)S(1)} %multiply_convert_fusion.8), channel_id=1, source_target_pairs={{0,8},{1,9},{2,10},{3,11},{4,12},{5,13},{6,14},{7,15},{8,0},{9,1},... | collective-permute-start | bytes 1572872 | tf_op jit(solution)/shard_map/ppermute | solution.py:12
  164.5 9.6 %collective-permute-start.4 = (bf16[256,1024]{1,0:T(8,128)(2,1)S(1)}, bf16[256,1024]{1,0:T(8,128)(2,1)S(1)}, u32[]{:S(2)}, u32[]{:S(2)}) collective-permute-start(bf16[256,1024]{1,0:T(8,128)(2,1)S(1)} %multiply_convert_fusion.7), channel_id=1, source_target_pairs={{0,16},{1,17},{2,18},{3,19},{4,20},{5,21},{6,22},{7,23},{8,24},{9,... | collective-permute-start | bytes 1572872 | tf_op jit(solution)/shard_map/ppermute | solution.py:12
  174.4 10.5 %collective-permute-start.5 = (bf16[256,1024]{1,0:T(8,128)(2,1)S(1)}, bf16[256,1024]{1,0:T(8,128)(2,1)S(1)}, u32[]{:S(2)}, u32[]{:S(2)}) collective-permute-start(bf16[256,1024]{1,0:T(8,128)(2,1)S(1)} %multiply_convert_fusion.6), channel_id=1, source_target_pairs={{0,32},{32,0},{64,96},{96,64},{1,33},{33,1},{65,97},{97,65},{2,34}... | collective-permute-start | bytes 1572872 | tf_op jit(solution)/shard_map/ppermute | solution.py:12
  185.1 13.2 %collective-permute-start.6 = (bf16[256,1024]{1,0:T(8,128)(2,1)S(1)}, bf16[256,1024]{1,0:T(8,128)(2,1)S(1)}, u32[]{:S(2)}, u32[]{:S(2)}) collective-permute-start(bf16[256,1024]{1,0:T(8,128)(2,1)S(1)} %multiply_convert_fusion.5), channel_id=1, source_target_pairs={{0,64},{32,96},{64,0},{96,32},{1,65},{33,97},{65,1},{97,33},{2,66}... | collective-permute-start | bytes 1572872 | tf_op jit(solution)/shard_map/ppermute | solution.py:12
where the time goes:
time: 200 us
  waiting for transfers between devices  131 us (66%)
  local copies, waits for them, and re-layouts  21.7 us (11%)
  starting transfers between devices  21.7 us (11%)
  matrix products  21.6 us (11%)
  other arithmetic  3.93 us (2%)
    ppermute x7, waiting for transfers between devices, partner_2(): lax.ppermute(shard, axis, [(i, i ^ 1 << distance) for i in range(lax.axis...  69.7 us
    all_to_all x1, waiting for transfers between devices, on_device(): lax.all_to_all(dosage, 'dev', split_axis=1, concat_axis=0, tiled=True)  61.1 us
    dot_general x1, matrix products, on_device(): jnp.dot(projected, hadamard_table(local_count), preferred_element_type=jn...  21.6 us
    all_to_all x1, starting transfers between devices, on_device(): lax.all_to_all(dosage, 'dev', split_axis=1, concat_axis=0, tiled=True)  11.4 us
    ppermute x7, starting transfers between devices, partner_2(): lax.ppermute(shard, axis, [(i, i ^ 1 << distance) for i in range(lax.axis...  10.2 us
    gather x1, local copies, waits for them, and re-layouts, on_device(): genotype = jnp.take(slots_all, variant_slot, axis=0)  7.7 us
    gather x1, local copies, waits for them, and re-layouts, on_device(): genotype = jnp.take(genotype, sample_perm % local_count, axis=1)  5.4 us
    all_to_all x1, local copies, waits for them, and re-layouts, on_device(): lax.all_to_all(dosage, 'dev', split_axis=1, concat_axis=0, tiled=True)  4.87 us
  transfers between devices with their start and end apart: 8, of which 8 were waited for; matrix products, arithmetic and copies ran while one was open for 0% of the time, Pallas kernels for 0%

commit v1 on v0

v1 whole, which is shorter than its diff:
```python
import math

import jax
import jax.numpy as jnp
from jax import lax
from jax.experimental import pallas as pl
from jax.experimental.pallas import tpu as pltpu
from jax.sharding import PartitionSpec as P

V = 1024
K = 256
SECTION = 1024
LOW = 256
HIGH = SECTION // LOW
CAP = 64
BF = jnp.bfloat16
F32 = jnp.float32


def iota(shape, axis):
    return lax.broadcasted_iota(jnp.int32, shape, axis)


def parity_sign(bits):
    bits = bits ^ (bits >> 4)
    bits = bits ^ (bits >> 2)
    bits = bits ^ (bits >> 1)
    return (1 - 2 * (bits & 1)).astype(F32)


def invert_kernel(perm_ref, sign_ref, out_ref):
    spot = perm_ref[...] & (SECTION - 1)
    where_is = (jnp.broadcast_to(spot, (SECTION, SECTION)) == iota((SECTION, SECTION), 0)).astype(F32).astype(BF)
    position = iota((8, SECTION), 1)
    negative = jnp.broadcast_to((sign_ref[...] < 0).astype(jnp.int32), (8, SECTION))
    digits = jnp.where(iota((8, SECTION), 0) == 0, position % LOW, position // LOW + HIGH * negative)
    found = lax.dot_general(digits.astype(F32).astype(BF), where_is, (((1,), (1,)), ((), ())), preferred_element_type=F32)
    found = found.astype(jnp.int32)
    out_ref[...] = found[0:1] + LOW * found[1:2]


def slot_kernel(slot_ref, proj_ref, out_ref):
    slot = slot_ref[...]
    target = (slot // 16 % 4) * 512 + slot // CAP * 16 + slot % 16
    chunk = 512
    proj = proj_ref[...]
    for c in range(4):
        hot = (jnp.broadcast_to(target, (chunk, V)) == iota((chunk, V), 0) + c * chunk).astype(F32).astype(BF)
        out_ref[c] = jnp.dot(hot, proj, preferred_element_type=F32).astype(BF)


def mix_kernel(place_ref, dos_hbm, code_ref, rows_ref, slot_ref, cen_ref, scl_ref, out_ref, dos, mix, sems):
    blocks = dos.shape[0]

    def fetch(b):
        return pltpu.make_async_copy(dos_hbm.at[:, pl.ds(b * SECTION, SECTION)], dos.at[b], sems.at[b])

    for b in range(blocks):
        fetch(b).start()

    mine = jnp.broadcast_to(slot_ref[...], (CAP, V)) == iota((CAP, V), 0) + place_ref[0] * CAP
    center = jnp.sum(jnp.where(mine, jnp.broadcast_to(cen_ref[...], (CAP, V)), 0.0), axis=1, keepdims=True)
    scale = jnp.sum(jnp.where(mine, jnp.broadcast_to(scl_ref[...], (CAP, V)), 0.0), axis=1, keepdims=True)
    low_iota = iota((LOW, LOW), 0).astype(F32).astype(BF)

    def place(b, carry):
        fetch(b).wait()
        acc = None
        for c in range(SECTION // LOW):
            cols = pl.ds(c * LOW, LOW)
            code = code_ref[pl.ds(b, 1), cols]
            low = (code & (LOW - 1)).astype(F32).astype(BF)
            high = jnp.broadcast_to(((code // LOW) & (HIGH - 1)).astype(F32).astype(BF), (CAP, LOW))
            flip = (1 - 2 * (code // SECTION)).astype(F32)
            signed = ((dos[b, :, cols].astype(F32) - center) * scale * flip).astype(BF)
            zero = jnp.zeros_like(signed)
            parts = [jnp.where(high == jnp.array(h, BF), signed, zero) for h in range(HIGH)]
            hot = jnp.where(jnp.broadcast_to(low, (LOW, LOW)) == low_iota, jnp.array(1, BF), jnp.array(0, BF))
            part = lax.dot_general(
                jnp.concatenate(parts, axis=0), hot, (((1,), (1,)), ((), ())), preferred_element_type=F32
            )
            acc = part if acc is None else acc + part
        mix[b] = acc
        return carry

    lax.fori_loop(0, blocks, place, 0)

    def cross(i, carry):
        top = pl.multiple_of(i * 8, 8)
        for c in range(LOW // 128):
            cols = pl.ds(c * 128, 128)
            vals = [mix[b, pl.ds(top, 8), cols] for b in range(blocks)]
            step = 1
            while step < blocks:
                nxt = list(vals)
                for b in range(blocks):
                    if not b & step:
                        nxt[b] = vals[b] + vals[b + step]
                        nxt[b + step] = vals[b] - vals[b + step]
                vals = nxt
                step *= 2
            for b in range(blocks):
                mix[b, pl.ds(top, 8), cols] = vals[b]
        return carry

    lax.fori_loop(0, HIGH * CAP // 8, cross, 0)

    lane = iota((16, 128), 1) // 32
    norm = 1.0 / math.sqrt(SECTION * blocks * 4)

    def sample(d, carry):
        row = rows_ref[pl.ds(d, 1), :] & (SECTION - 1)
        table = parity_sign(jnp.broadcast_to(row & (LOW - 1), (LOW, 128)) & iota((LOW, 128), 0)).astype(BF)
        raw = jnp.dot(mix[d].astype(BF), table, preferred_element_type=F32)
        top = row // LOW
        s1 = (1 - 2 * (top & 1)).astype(F32)
        s2 = (1 - 2 * (top // 2)).astype(F32)
        w = (raw[0:CAP] + s1 * raw[CAP : 2 * CAP]) + s2 * (raw[2 * CAP : 3 * CAP] + s1 * raw[3 * CAP :])
        w = w * norm
        for g in range(4):
            out = None
            for q in range(4):
                piece = w[16 * q : 16 * q + 16]
                if q != g:
                    piece = pltpu.roll(piece, 32 * ((q - g) % 4), 1)
                out = piece if out is None else jnp.where(lane == q, piece, out)
            out_ref[g, d] = out.astype(BF)
        return carry

    lax.fori_loop(0, blocks, sample, 0)


def finish_kernel(place_ref, got_ref, proj_ref, out_ref):
    files = got_ref.shape[1]
    group = place_ref[0]
    odd1 = (1 - 2 * (group % 2)).astype(F32)
    odd2 = (1 - 2 * (group // 2)).astype(F32)
    g = [got_ref[i].astype(F32) for i in range(4)]
    total = (g[0] + odd1 * g[1]) + odd2 * (g[2] + odd1 * g[3])
    total = total.reshape(files * 16, 128).astype(BF)
    out = None
    for q in range(4):
        full = lax.dot_general(total, proj_ref[q], (((0,), (0,)), ((), ())), preferred_element_type=F32)
        part = full[32 * q : 32 * q + 32]
        out = part if out is None else out + part
    out_ref[...] = out


def vmem(n):
    return [pl.BlockSpec(memory_space=pltpu.VMEM)] * n


def smem():
    return pl.BlockSpec(memory_space=pltpu.SMEM)


def on_device(
    dosage, variant_slot, center, variant_scale, sample_signs, sample_perm, sample_rows, projection
):
    groups, devs = lax.axis_size("grp"), lax.axis_size("dev")
    both = ("grp", "dev")
    group, dev = lax.axis_index("grp"), lax.axis_index("dev")
    code = pl.pallas_call(
        invert_kernel,
        out_shape=jax.ShapeDtypeStruct((1, SECTION), jnp.int32),
        in_specs=vmem(2),
        out_specs=pl.BlockSpec(memory_space=pltpu.VMEM),
    )(sample_perm[None], sample_signs[None])
    slot_proj = pl.pallas_call(
        slot_kernel,
        out_shape=jax.ShapeDtypeStruct((4, 512, K), BF),
        in_specs=vmem(2),
        out_specs=pl.BlockSpec(memory_space=pltpu.VMEM),
    )(variant_slot[None], projection)
    send = jnp.concatenate([code, sample_rows[None]], axis=1)
    send = jnp.broadcast_to(send, (groups * devs, SECTION + 32))
    got = lax.all_to_all(send, both, 0, 0, tiled=True)
    codes = lax.dynamic_slice(got, (group * devs, 0), (devs, SECTION))
    rows = got[:, SECTION:].reshape(groups, devs, 32).transpose(1, 0, 2).reshape(devs, groups * 32)
    mixed = pl.pallas_call(
        mix_kernel,
        out_shape=jax.ShapeDtypeStruct((groups, devs, 16, 128), BF),
        in_specs=[smem(), pl.BlockSpec(memory_space=pl.ANY)] + vmem(5),
        out_specs=pl.BlockSpec(memory_space=pltpu.VMEM),
        scratch_shapes=[
            pltpu.VMEM((devs, CAP, SECTION), BF),
            pltpu.VMEM((devs, HIGH * CAP, LOW), F32),
            pltpu.SemaphoreType.DMA((devs,)),
        ],
    )(dev[None], dosage, codes, rows, variant_slot[None], center[None], variant_scale[None])
    mixed = mixed.reshape(groups * devs, 16, 128)
    got = lax.all_to_all(mixed, both, 0, 0, tiled=True).reshape(groups, devs, 16, 128)
    return pl.pallas_call(
        finish_kernel,
        out_shape=jax.ShapeDtypeStruct((32, K), F32),
        in_specs=[smem()] + vmem(2),
        out_specs=pl.BlockSpec(memory_space=pltpu.VMEM),
    )(group[None], got, slot_proj)


def solution(mesh):
    return jax.shard_map(
        on_device,
        mesh=mesh,
        in_specs=(
            P("dev", "grp"),
            P(),
            P(),
            P(),
            P(("grp", "dev")),
            P(("grp", "dev")),
            P(("grp", "dev")),
            P(),
        ),
        out_specs=P(("grp", "dev"), None),
        check_vma=False,
    )
```

time: 200 us -> 80.4 us (0.40)
  waiting for transfers between devices: 131 us -> 25.1 us
  Pallas kernels: 0 us -> 33.9 us
  matrix products: 21.6 us -> 0 us
  local copies, waits for them, and re-layouts: 21.7 us -> 4.4 us
  starting transfers between devices: 21.7 us -> 15.8 us
  other arithmetic: 3.93 us -> 0.72 us
    ppermute x7 -> x0, waiting for transfers between devices: 69.7 us -> none  [partner_2(): lax.ppermute(shard, axis, [(i, i ^ 1 << distance) for i in range(lax.axis...]
    all_to_all x1 -> x2, waiting for transfers between devices: 61.1 us -> 25.1 us  [the longest x1 14.5 us: on_device(): got = lax.all_to_all(send, both, 0, 0, tiled=True)]
    pallas_call x0 -> x4, Pallas kernels: none -> 33.9 us  [the longest x1 26.3 us: on_device(): pl.pallas_call(mix_kernel, out_shape=jax.ShapeDtypeStruct((groups, devs,...]
    dot_general x1 -> x0, matrix products: 21.6 us -> none  [on_device(): jnp.dot(projected, hadamard_table(local_count), preferred_element_type=jn...]
    gather x3 -> x0, local copies, waits for them, and re-layouts: 13.7 us -> none  [the longest x1 7.7 us: on_device(): genotype = jnp.take(slots_all, variant_slot, axis=0)]
    ppermute x7 -> x0, starting transfers between devices: 10.2 us -> none  [partner_2(): lax.ppermute(shard, axis, [(i, i ^ 1 << distance) for i in range(lax.axis...]
    all_to_all x1 -> x2, starting transfers between devices: 11.4 us -> 15.8 us  [the longest x1 11.5 us: on_device(): got = lax.all_to_all(send, both, 0, 0, tiled=True)]
    all_to_all x1, local copies, waits for them, and re-layouts: 4.87 us -> 0.9 us  [on_device(): got = lax.all_to_all(send, both, 0, 0, tiled=True)]
  transfers between devices with their start and end apart: 8 -> 2, of which waited for: 8 -> 2; matrix products, arithmetic and copies ran while one was open for 0% -> 0% of each run, Pallas kernels for 0% -> 4%
where the time goes in v1:
time: 80.4 us; the launch traced here: 80 us
  Pallas kernels  33.9 us (42%)
  waiting for transfers between devices  25.1 us (31%)
  starting transfers between devices  15.8 us (20%)
  local copies, waits for them, and re-layouts  4.4 us (5%)
    pallas_call x1, Pallas kernels, on_device(): pl.pallas_call(mix_kernel, out_shape=jax.ShapeDtypeStruct((groups, devs,...  26.3 us
    all_to_all x1, waiting for transfers between devices, on_device(): got = lax.all_to_all(send, both, 0, 0, tiled=True)  14.5 us
    all_to_all x1, starting transfers between devices, on_device(): got = lax.all_to_all(send, both, 0, 0, tiled=True)  11.5 us
    all_to_all x1, waiting for transfers between devices, on_device(): lax.all_to_all(mixed, both, 0, 0, tiled=True).reshape(groups, devs, 16, 128)  10.5 us
    all_to_all x1, starting transfers between devices, on_device(): lax.all_to_all(mixed, both, 0, 0, tiled=True).reshape(groups, devs, 16, 128)  4.35 us
    pallas_call x1, Pallas kernels, on_device(): pl.pallas_call(slot_kernel, out_shape=jax.ShapeDtypeStruct((4, 512, K), B...  3.28 us
    pallas_call x1, Pallas kernels, on_device(): pl.pallas_call(finish_kernel, out_shape=jax.ShapeDtypeStruct((32, K), F32...  2.38 us
    pallas_call x1, Pallas kernels, on_device(): pl.pallas_call(invert_kernel, out_shape=jax.ShapeDtypeStruct((1, SECTION)...  1.97 us
  transfers between devices with their start and end apart: 2, of which 2 were waited for; matrix products, arithmetic and copies ran while one was open for 0% of the time, Pallas kernels for 4%

profile of v1, /device:TPU:1, one launch (start us, length us, event | category | flops | bytes accessed | tf_op | source)
XLA Modules:
  0.0 80.0 jit_solution(4498512740793889860)
XLA Ops:
  0.0 2.0 %shard_map.82 = s32[1,1024]{1,0:T(1,128)} custom-call(s32[1,1024]{1,0:T(1,128)} %bitcast.24, s32[1,1024]{1,0:T(1,128)} %bitcast.25), custom_call_target="tpu_custom_call" | custom-call | tf_op jit(solution)/shard_map/pallas_call | solution.py:163
  2.0 0.7 add_reduce_fusion
  2.7 1.1 %broadcast_in_dim.35 = s32[128,1,1056]{2,1,0:T(1,128)} broadcast(s32[1056]{0:T(1024)S(1)} %add_reduce_fusion), dimensions={2} | broadcast | bytes 544896 | tf_op jit(solution)/shard_map/broadcast_in_dim | solution.py:176
  3.8 11.5 %all-to-all-start = ((s32[128,1,1056]{2,1,0:T(1,128)}), s32[128,1,1056]{2,1,0:T(1,128)S(1)}, u32[]{:S(2)}, u32[]{:S(2)}) async-start(s32[128,1,1056]{2,1,0:T(1,128)} %broadcast_in_dim.35), calls=%async_computation | async-start | bytes 1179648 | tf_op jit(solution)/shard_map/all_to_all | solution.py:177
  15.3 14.5 %all-to-all-done = s32[128,1,1056]{2,1,0:T(1,128)S(1)} async-done(((s32[128,1,1056]{2,1,0:T(1,128)}), s32[128,1,1056]{2,1,0:T(1,128)S(1)}, u32[]{:S(2)}, u32[]{:S(2)}) %all-to-all-start) | async-done | bytes 540704 | tf_op jit(solution)/shard_map/all_to_all | solution.py:177
  29.8 0.9 %copy.13 = s32[128,1,1056]{0,2,1:T(8,128)S(1)} copy(s32[128,1,1056]{2,1,0:T(1,128)S(1)} %all-to-all-done) | data formatting | bytes 1081344 | tf_op jit(solution)/shard_map/all_to_all | solution.py:177
  30.8 0.7 copy.17
  31.5 0.1 reshape.19
  31.6 0.1 copy.14
  31.6 0.7 reshape.20.rows_ref
  32.4 26.3 %shard_map.83 = bf16[4,32,16,128]{3,2,1,0:T(8,128)(2,1)} custom-call(s32[1]{0:T(128)} %bitcast.1.place_ref, bf16[64,32768]{1,0:T(8,128)(2,1)} %dos_hbm.1, s32[32,1024]{1,0:T(8,128)} %bitcast.20, s32[32,128]{1,0:T(8,128)} %reshape.20.rows_ref, s32[1,1024]{1,0:T(1,128)} %bitcast.22, f32[1,1024]{1,0:T(1,128)} %bitcast.26, f32[1,1024]{1,0:T(1,128)} %bitcast.27), custom_call_target="tpu_custom_call" | custom-call | tf_op jit(solution)/shard_map/pallas_call | solution.py:180
  58.7 4.3 %all-to-all-start.1 = ((bf16[128,16,128]{2,1,0:T(8,128)(2,1)}), bf16[128,16,128]{2,1,0:T(8,128)(2,1)S(1)}, u32[]{:S(2)}, u32[]{:S(2)}) async-start(bf16[128,16,128]{2,1,0:T(8,128)(2,1)} %bitcast.17), calls=%async_computation.1 | async-start | bytes 1048576 | tf_op jit(solution)/shard_map/all_to_all | solution.py:192
  63.0 3.3 %shard_map.84.proj_ref = bf16[4,512,256]{2,1,0:T(8,128)(2,1)} custom-call(s32[1,1024]{1,0:T(1,128)} %bitcast.23, bf16[1024,256]{1,0:T(8,128)(2,1)} %proj_ref.1), custom_call_target="tpu_custom_call" | custom-call | tf_op jit(solution)/shard_map/pallas_call | solution.py:169
  66.3 10.5 %all-to-all-done.1 = bf16[128,16,128]{2,1,0:T(8,128)(2,1)S(1)} async-done(((bf16[128,16,128]{2,1,0:T(8,128)(2,1)}), bf16[128,16,128]{2,1,0:T(8,128)(2,1)S(1)}, u32[]{:S(2)}, u32[]{:S(2)}) %all-to-all-start.1) | async-done | bytes 524320 | tf_op jit(solution)/shard_map/all_to_all | solution.py:192
  76.8 0.0 copy-start
  76.8 0.8 copy-done
  77.6 2.4 %shard_map.85 = f32[32,256]{1,0:T(8,128)} custom-call(s32[1]{0:T(128)} %bitcast.place_ref, bf16[4,32,16,128]{3,2,1,0:T(8,128)(2,1)} %bitcast.18, bf16[4,512,256]{2,1,0:T(8,128)(2,1)} %shard_map.84.proj_ref), custom_call_target="tpu_custom_call" | custom-call | tf_op jit(solution)/shard_map/pallas_call | solution.py:193
  (2 shorter events, 0.0 us)
Async XLA Ops:
  3.8 26.0 %all-to-all-start = ((s32[128,1,1056]{2,1,0:T(1,128)}), s32[128,1,1056]{2,1,0:T(1,128)S(1)}, u32[]{:S(2)}, u32[]{:S(2)}) async-start(s32[128,1,1056]{2,1,0:T(1,128)} %broadcast_in_dim.35), calls=%async_computation | async-start | bytes 1179648 | tf_op jit(solution)/shard_map/all_to_all | solution.py:177
  58.7 18.2 %all-to-all-start.1 = ((bf16[128,16,128]{2,1,0:T(8,128)(2,1)}), bf16[128,16,128]{2,1,0:T(8,128)(2,1)S(1)}, u32[]{:S(2)}, u32[]{:S(2)}) async-start(bf16[128,16,128]{2,1,0:T(8,128)(2,1)} %bitcast.17), calls=%async_computation.1 | async-start | bytes 1048576 | tf_op jit(solution)/shard_map/all_to_all | solution.py:192
  76.8 0.8 copy-start

commit v2 on v1

v2 whole, which is shorter than its diff:
```python
import math

import jax
import jax.numpy as jnp
from jax import lax
from jax.experimental import pallas as pl
from jax.experimental.pallas import tpu as pltpu
from jax.sharding import PartitionSpec as P

V = 1024
K = 256
SECTION = 1024
LOW = 128
HIGH = SECTION // LOW
CAP = 64
LANES = 128
UNROLL1, UNROLL2, UNROLL3 = 4, 1, 4
BF = jnp.bfloat16
F32 = jnp.float32
NT = (((1,), (1,)), ((), ()))
TN = (((0,), (0,)), ((), ()))


def iota(shape, axis):
    return lax.broadcasted_iota(jnp.int32, shape, axis)


def small(ints):
    return ints.astype(F32).astype(BF)


def invert_kernel(place_ref, perm_ref, sign_ref, rows_ref, out_ref):
    spot = perm_ref[...] & (SECTION - 1)
    row = iota((2 * HIGH, SECTION), 0)
    position = iota((2 * HIGH, SECTION), 1)
    digit = jnp.where(row < HIGH, position % LOW, position // LOW + HIGH * (sign_ref[...] < 0).astype(jnp.int32))
    digit = jnp.where(spot // LOW == row % HIGH, digit, 0)
    hot = jnp.where(small(spot % LOW) == small(iota((LOW, SECTION), 0)), jnp.array(1, BF), jnp.array(0, BF))
    found = lax.dot_general(small(digit), hot, NT, preferred_element_type=F32).astype(jnp.int32)
    code = found[:HIGH] + LOW * found[HIGH:]
    lane = iota((1, LANES), 1)
    mine = jnp.where(lane // 32 == place_ref[0], rows_ref[...] & (SECTION - 1), 0)
    count = out_ref.shape[0]
    for h in range(HIGH):
        out_ref[:, :, h * LANES : (h + 1) * LANES] = jnp.broadcast_to(code[h : h + 1][None], (count, 1, LANES))
    out_ref[:, :, SECTION:] = jnp.broadcast_to(mine[None], (count, 1, LANES))


def ready_kernel(place_ref, dos_ref, slot_ref, cen_ref, scl_ref, proj_ref, out_ref, gain_ref, had_ref, sp_ref, cen_col):
    step = pl.program_id(0)

    @pl.when(step == 0)
    def _():
        mine = jnp.broadcast_to(slot_ref[...], (CAP, V)) == iota((CAP, V), 0) + place_ref[0] * CAP
        center = jnp.sum(jnp.where(mine, jnp.broadcast_to(cen_ref[...], (CAP, V)), 0.0), axis=1, keepdims=True)
        scale = jnp.sum(jnp.where(mine, jnp.broadcast_to(scl_ref[...], (CAP, V)), 0.0), axis=1, keepdims=True)
        cen_col[...] = jnp.broadcast_to(center, (CAP, LANES))
        gain_ref[...] = jnp.broadcast_to(scale, (CAP, LANES))
        bits = iota((LOW, LOW), 0) & iota((LOW, LOW), 1)
        bits = bits ^ (bits >> 4)
        bits = bits ^ (bits >> 2)
        bits = bits ^ (bits >> 1)
        had_ref[...] = small(1 - 2 * (bits & 1))

    center = cen_col[:, 0:1]
    for i in range(out_ref.shape[0]):
        out_ref[i] = (dos_ref[:, i * SECTION : (i + 1) * SECTION].astype(F32) - center).astype(BF)

    rows = sp_ref.shape[0]
    slot = slot_ref[...]
    target = (slot // 16 % 4) * 512 + slot // CAP * 16 + slot % 16
    hot = (jnp.broadcast_to(target, (rows, V)) == iota((rows, V), 0) + step * rows).astype(F32).astype(BF)
    sp_ref[...] = jnp.dot(hot, proj_ref[...], preferred_element_type=F32).astype(BF)


def mix_kernel(place_ref, xs_ref, got_ref, gain_ref, had_ref, out_ref, mix, tables):
    blocks = xs_ref.shape[0]
    group = place_ref[0]
    norm = 1.0 / math.sqrt(SECTION * blocks * 4)
    one, zero = jnp.array(1, BF), jnp.array(0, BF)

    def place(b, carry):
        code = got_ref[group * blocks + b, :, 0:SECTION]
        low = jnp.broadcast_to(small(code & (LOW - 1)), (LOW, SECTION))
        flip = jnp.broadcast_to(small(1 - 2 * (code // SECTION)), (LOW, SECTION))
        high = jnp.broadcast_to(small((code // LOW) & (HIGH - 1)), (CAP, SECTION))
        shifted = xs_ref[b]
        parts = [jnp.where(high == jnp.array(h, BF), shifted, zero) for h in range(HIGH)]
        hot = jnp.where(low == small(iota((LOW, SECTION), 0)), flip, zero)
        spot = lax.dot_general(jnp.concatenate(parts, axis=0), hot, NT, preferred_element_type=F32).astype(BF)
        mix[b] = spot.reshape(mix.shape[1:])
        row = sum(got_ref[g * blocks + b, :, SECTION:] for g in range(4))
        hot = jnp.where(jnp.broadcast_to(small(row & (LOW - 1)), (LOW, LANES)) == small(iota((LOW, LANES), 0)), one, zero)
        tables[b] = jnp.dot(had_ref[...], hot, preferred_element_type=F32).astype(BF)
        return carry

    lax.fori_loop(0, blocks, place, 0, unroll=UNROLL1)

    def cross(i, carry):
        vals = [mix[b, i] for b in range(blocks)]
        step = 1
        while step < blocks:
            nxt = list(vals)
            for b in range(blocks):
                if not b & step:
                    nxt[b] = vals[b] + vals[b + step]
                    nxt[b + step] = vals[b] - vals[b + step]
            vals = nxt
            step *= 2
        for b in range(blocks):
            mix[b, i] = vals[b]
        return carry

    lax.fori_loop(0, mix.shape[1], cross, 0, unroll=UNROLL2)

    lane = iota((16, LANES), 1) // 32
    gain = gain_ref[...] * norm

    def sample(d, carry):
        raw = jnp.dot(mix[d].reshape(HIGH * CAP, LOW), tables[d], preferred_element_type=F32)
        parts = [raw[h * CAP : (h + 1) * CAP] for h in range(HIGH)]
        top = sum(got_ref[g * blocks + d, :, SECTION:] for g in range(4)) // LOW
        while len(parts) > 1:
            sign = (1 - 2 * (top & 1)).astype(F32)
            parts = [parts[i] + sign * parts[i + 1] for i in range(0, len(parts), 2)]
            top = top // 2
        w = parts[0] * gain
        spun = [w[16 * q : 16 * q + 16] for q in range(4)]
        spun = [spun[0]] + [pltpu.roll(spun[q], 32 * q, 1) for q in range(1, 4)]
        for g in range(4):
            out = spun[0]
            for q in range(1, 4):
                out = jnp.where(lane == (g + q) % 4, spun[q], out)
            out_ref[g, d] = out.astype(BF)
        return carry

    lax.fori_loop(0, blocks, sample, 0, unroll=UNROLL3)


def finish_kernel(place_ref, got_ref, proj_ref, out_ref):
    files = got_ref.shape[1]
    group = place_ref[0]
    odd1 = (1 - 2 * (group % 2)).astype(F32)
    odd2 = (1 - 2 * (group // 2)).astype(F32)
    g = [got_ref[i].astype(F32) for i in range(4)]
    total = (g[0] + odd1 * g[1]) + odd2 * (g[2] + odd1 * g[3])
    total = total.reshape(files * 16, 128).astype(BF)
    out = None
    for q in range(4):
        full = lax.dot_general(total, proj_ref[(q + 4 - group) % 4], TN, preferred_element_type=F32)
        part = full[32 * q : 32 * q + 32]
        out = part if out is None else out + part
    out_ref[...] = out


def vmem(n):
    return [pl.BlockSpec(memory_space=pltpu.VMEM)] * n


def limit(mib):
    return pltpu.CompilerParams(vmem_limit_bytes=mib << 20)


def smem():
    return pl.BlockSpec(memory_space=pltpu.SMEM)


def on_device(
    dosage, variant_slot, center, variant_scale, sample_signs, sample_perm, sample_rows, projection
):
    groups, devs = lax.axis_size("grp"), lax.axis_size("dev")
    both = ("grp", "dev")
    group, dev = lax.axis_index("grp"), lax.axis_index("dev")
    send = pl.pallas_call(
        invert_kernel,
        out_shape=jax.ShapeDtypeStruct((groups * devs, 1, SECTION + LANES), jnp.int32),
        in_specs=[smem()] + vmem(3),
        out_specs=pl.BlockSpec(memory_space=pltpu.VMEM),
        compiler_params=limit(8),
    )(group[None], sample_perm[None], sample_signs[None], jnp.tile(sample_rows, 4)[None])
    steps = 8
    per = devs // steps
    xs, gain, had, slot_proj = pl.pallas_call(
        ready_kernel,
        grid=(steps,),
        out_shape=(
            jax.ShapeDtypeStruct((devs, CAP, SECTION), BF),
            jax.ShapeDtypeStruct((CAP, LANES), F32),
            jax.ShapeDtypeStruct((LOW, LOW), BF),
            jax.ShapeDtypeStruct((devs * CAP, K), BF),
        ),
        in_specs=[
            smem(),
            pl.BlockSpec((CAP, per * SECTION), lambda i: (0, i)),
            pl.BlockSpec((1, V), lambda i: (0, 0)),
            pl.BlockSpec((1, V), lambda i: (0, 0)),
            pl.BlockSpec((1, V), lambda i: (0, 0)),
            pl.BlockSpec((V, K), lambda i: (0, 0)),
        ],
        out_specs=(
            pl.BlockSpec((per, CAP, SECTION), lambda i: (i, 0, 0)),
            pl.BlockSpec((CAP, LANES), lambda i: (0, 0)),
            pl.BlockSpec((LOW, LOW), lambda i: (0, 0)),
            pl.BlockSpec((devs * CAP // steps, K), lambda i: (i, 0)),
        ),
        scratch_shapes=[pltpu.VMEM((CAP, LANES), F32)],
        compiler_params=limit(12),
    )(dev[None], dosage, variant_slot[None], center[None], variant_scale[None], projection)
    got = lax.all_to_all(send, both, 0, 0, tiled=True)
    mixed = pl.pallas_call(
        mix_kernel,
        out_shape=jax.ShapeDtypeStruct((groups, devs, 16, LANES), BF),
        in_specs=[smem()] + vmem(4),
        out_specs=pl.BlockSpec(memory_space=pltpu.VMEM),
        compiler_params=limit(24),
        scratch_shapes=[
            pltpu.VMEM((devs, HIGH * CAP // 16, 16, LOW), BF),
            pltpu.VMEM((devs, LOW, LANES), BF),
        ],
    )(group[None], xs, got, gain, had)
    mixed = mixed.reshape(groups * devs, 16, 128)
    got = lax.all_to_all(mixed, both, 0, 0, tiled=True).reshape(groups, devs, 16, 128)
    return pl.pallas_call(
        finish_kernel,
        out_shape=jax.ShapeDtypeStruct((32, K), F32),
        in_specs=[smem()] + vmem(2),
        out_specs=pl.BlockSpec(memory_space=pltpu.VMEM),
        compiler_params=limit(8),
    )(group[None], got, slot_proj.reshape(4, devs * 16, K))


def solution(mesh):
    return jax.shard_map(
        on_device,
        mesh=mesh,
        in_specs=(
            P("dev", "grp"),
            P(),
            P(),
            P(),
            P(("grp", "dev")),
            P(("grp", "dev")),
            P(("grp", "dev")),
            P(),
        ),
        out_specs=P(("grp", "dev"), None),
        check_vma=False,
    )
```

time: 80.4 us -> 68 us (0.85)
  waiting for transfers between devices: 25.1 us -> 4.08 us
  blocking collectives: 0 us -> 19.3 us
  Pallas kernels: 33.9 us -> 21.1 us
  local copies, waits for them, and re-layouts: 4.4 us -> 11.5 us
  starting transfers between devices: 15.8 us -> 11.5 us
    all_to_all x0 -> x1, blocking collectives: none -> 19.3 us  [on_device(): lax.all_to_all(mixed, both, 0, 0, tiled=True).reshape(groups, devs, 16, 128)]
    pallas_call x1, Pallas kernels: 26.3 us -> 15.6 us  [on_device(): pl.pallas_call(mix_kernel, out_shape=jax.ShapeDtypeStruct((groups, devs,...]
    all_to_all x1 -> x0, waiting for transfers between devices: 10.5 us -> none  [on_device(): lax.all_to_all(mixed, both, 0, 0, tiled=True).reshape(groups, devs, 16, 128)]
    all_to_all x1, waiting for transfers between devices: 14.5 us -> 4.08 us  [on_device(): got = lax.all_to_all(send, both, 0, 0, tiled=True)]
    unnamed x3 -> x18, local copies, waits for them, and re-layouts: 1.47 us -> 10.8 us
    all_to_all x1 -> x0, starting transfers between devices: 4.35 us -> none  [on_device(): lax.all_to_all(mixed, both, 0, 0, tiled=True).reshape(groups, devs, 16, 128)]
    pallas_call x1, Pallas kernels: 2.38 us -> 1 us  [on_device(): pl.pallas_call(finish_kernel, out_shape=jax.ShapeDtypeStruct((32, K), F32...]
    broadcast_in_dim x1 -> x0, local copies, waits for them, and re-layouts: 1.11 us -> none  [on_device(): send = jnp.broadcast_to(send, (groups * devs, SECTION + 32))]
  transfers between devices with their start and end apart: 2 -> 1, of which waited for: 2 -> 1; matrix products, arithmetic and copies ran while one was open for 0% -> 0% of each run, Pallas kernels for 4% -> 5%
where the time goes in v2:
time: 68 us; the launch traced here: 67.5 us
  Pallas kernels  21.1 us (31%)
  blocking collectives  19.3 us (28%)
  local copies, waits for them, and re-layouts  11.5 us (17%)
  starting transfers between devices  11.5 us (17%)
  waiting for transfers between devices  4.08 us (6%)
    all_to_all x1, blocking collectives, on_device(): lax.all_to_all(mixed, both, 0, 0, tiled=True).reshape(groups, devs, 16, 128)  19.3 us
    pallas_call x1, Pallas kernels, on_device(): pl.pallas_call(mix_kernel, out_shape=jax.ShapeDtypeStruct((groups, devs,...  15.6 us
    all_to_all x1, starting transfers between devices, on_device(): got = lax.all_to_all(send, both, 0, 0, tiled=True)  11.5 us
    unnamed x18, local copies, waits for them, and re-layouts  10.8 us
    all_to_all x1, waiting for transfers between devices, on_device(): got = lax.all_to_all(send, both, 0, 0, tiled=True)  4.08 us
    pallas_call x1, Pallas kernels, on_device(): pl.pallas_call(ready_kernel, grid=(steps,), out_shape=(jax.ShapeDtypeStru...  3.19 us
  transfers between devices with their start and end apart: 1, of which 1 were waited for; matrix products, arithmetic and copies ran while one was open for 0% of the time, Pallas kernels for 5%

profile of v2, /device:TPU:1, one launch (start us, length us, event | category | flops | bytes accessed | tf_op | source)
XLA Modules:
  0.0 67.5 jit_solution(13905684110795727594)
XLA Ops:
  0.0 0.7 tile.2
  0.7 0.1 broadcast_in_dim_tile.3.rows_ref
  0.7 0.0 copy-start.4
  0.7 0.7 %copy-done.4 = s32[1024]{0:T(1024)S(1)} copy-done((s32[1024]{0:T(1024)S(1)}, s32[1024]{0:T(1024)}, u32[]{:S(2)}) %copy-start.4) | copy-done | bytes 4120
  1.4 0.0 copy-start.5
  1.4 0.7 %copy-done.5 = s32[1024]{0:T(1024)S(1)} copy-done((s32[1024]{0:T(1024)S(1)}, s32[1024]{0:T(1024)}, u32[]{:S(2)}) %copy-start.5) | copy-done | bytes 4120
  2.1 1.3 %shard_map.83 = s32[128,1,1152]{2,1,0:T(1,128)} custom-call(s32[1]{0:T(128)} %bitcast.place_ref, s32[1,1024]{1,0:T(1,128)S(1)} %bitcast.13, s32[1,1024]{1,0:T(1,128)S(1)} %bitcast.14, s32[1,128]{1,0:T(1,128)S(1)} %broadcast_in_dim_tile.3.rows_ref), custom_call_target="tpu_custom_call" | custom-call | tf_op jit(solution)/shard_map/pallas_call | solution.py:174
  3.4 11.5 %all-to-all-start = ((s32[128,1,1152]{2,1,0:T(1,128)}), s32[128,1,1152]{2,1,0:T(1,128)S(1)}, u32[]{:S(2)}, u32[]{:S(2)}) async-start(s32[128,1,1152]{2,1,0:T(1,128)} %shard_map.83), calls=%async_computation | async-start | bytes 1179648 | tf_op jit(solution)/shard_map/all_to_all | solution.py:209
  14.9 0.0 copy-start
  14.9 2.2 %copy-done = bf16[64,32768]{1,0:T(8,128)(2,1)S(1)} copy-done((bf16[64,32768]{1,0:T(8,128)(2,1)S(1)}, bf16[64,32768]{1,0:T(8,128)(2,1)}, u32[]{:S(2)}) %copy-start) | copy-done | bytes 4194328
  17.1 0.0 copy-start.3
  17.1 1.0 %copy-done.3 = bf16[1024,256]{1,0:T(8,128)(2,1)S(1)} copy-done((bf16[1024,256]{1,0:T(8,128)(2,1)S(1)}, bf16[1024,256]{1,0:T(8,128)(2,1)}, u32[]{:S(2)}) %copy-start.3) | copy-done | bytes 524312
  18.1 0.0 copy-start.6
  18.2 0.7 %copy-done.6 = s32[1024]{0:T(1024)S(1)} copy-done((s32[1024]{0:T(1024)S(1)}, s32[1024]{0:T(1024)}, u32[]{:S(2)}) %copy-start.6) | copy-done | bytes 4120
  18.8 0.0 copy-start.7
  18.8 0.7 %copy-done.7 = f32[1024]{0:T(1024)S(1)} copy-done((f32[1024]{0:T(1024)S(1)}, f32[1024]{0:T(1024)}, u32[]{:S(2)}) %copy-start.7) | copy-done | bytes 4120
  19.5 0.0 copy-start.8
  19.5 0.7 %copy-done.8 = f32[1024]{0:T(1024)S(1)} copy-done((f32[1024]{0:T(1024)S(1)}, f32[1024]{0:T(1024)}, u32[]{:S(2)}) %copy-start.8) | copy-done | bytes 4120
  20.2 3.2 %shard_map.82 = (bf16[32,64,1024]{2,1,0:T(8,128)(2,1)S(1)}, f32[64,128]{1,0:T(8,128)S(1)}, bf16[128,128]{1,0:T(8,128)(2,1)S(1)}, bf16[2048,256]{1,0:T(8,128)(2,1)S(1)}) custom-call(s32[1]{0:T(128)} %bitcast.1.place_ref, bf16[64,32768]{1,0:T(8,128)(2,1)S(1)} %copy-done, s32[1,1024]{1,0:T(1,128)S(1)} %bitcast.15, f32[1,1024]{1,0:T(1,128)S(1)} %bitcast.16, ...), custom_call_target="tpu_custom_call" | custom-call | tf_op jit(solution)/shard_map/pallas_call | solution.py:183
  23.4 0.0 copy-start.1
  23.4 1.9 %copy-done.1 = bf16[32,64,1024]{2,1,0:T(8,128)(2,1)} copy-done((bf16[32,64,1024]{2,1,0:T(8,128)(2,1)}, bf16[32,64,1024]{2,1,0:T(8,128)(2,1)S(1)}, u32[]{:S(2)}) %copy-start.1) | copy-done | bytes 4194328
  25.4 4.1 %all-to-all-done.got_ref = s32[128,1,1152]{2,1,0:T(1,128)S(1)} async-done(((s32[128,1,1152]{2,1,0:T(1,128)}), s32[128,1,1152]{2,1,0:T(1,128)S(1)}, u32[]{:S(2)}, u32[]{:S(2)}) %all-to-all-start) | async-done | bytes 589856 | tf_op jit(solution)/shard_map/all_to_all | solution.py:209
  29.4 0.0 copy-start.2
  29.4 2.2 %copy-done.2 = bf16[32,64,1024]{2,1,0:T(8,128)(2,1)S(1)} copy-done((bf16[32,64,1024]{2,1,0:T(8,128)(2,1)S(1)}, bf16[32,64,1024]{2,1,0:T(8,128)(2,1)}, u32[]{:S(2)}) %copy-start.2) | copy-done | bytes 4194328
  31.6 15.6 %shard_map.84 = bf16[4,32,16,128]{3,2,1,0:T(8,128)(2,1)S(1)} custom-call(s32[1]{0:T(128)} %bitcast.place_ref, bf16[32,64,1024]{2,1,0:T(8,128)(2,1)S(1)} %copy-done.2, s32[128,1,1152]{2,1,0:T(1,128)S(1)} %all-to-all-done.got_ref, f32[64,128]{1,0:T(8,128)S(1)} %get-tuple-element.10.gain_ref, bf16[128,128]{1,0:T(8,128)(2,1)S(1)} %get-tuple-element.11.had_ref), custom_call_target="tpu_custom_call" | custom-call | tf_op jit(solution)/shard_map/pallas_call | solution.py:210
  47.2 19.3 %all_to_all.10 = bf16[128,16,128]{2,1,0:T(8,128)(2,1)S(1)} all-to-all(bf16[128,16,128]{2,1,0:T(8,128)(2,1)S(1)} %bitcast.11), channel_id=1, replica_groups=mesh['grp'=4,'dev'=32] {'grp','dev'}, dimensions={0} | all-to-all | bytes 1048576 | tf_op jit(solution)/shard_map/all_to_all | solution.py:222
  66.5 1.0 %shard_map.85 = f32[32,256]{1,0:T(8,128)} custom-call(s32[1]{0:T(128)} %bitcast.place_ref, bf16[4,32,16,128]{3,2,1,0:T(8,128)(2,1)S(1)} %bitcast.10, bf16[4,512,256]{2,1,0:T(8,128)(2,1)S(1)} %bitcast.12), custom_call_target="tpu_custom_call" | custom-call | tf_op jit(solution)/shard_map/pallas_call | solution.py:223
Async XLA Ops:
  0.7 0.7 %copy-start.4 = (s32[1024]{0:T(1024)S(1)}, s32[1024]{0:T(1024)}, u32[]{:S(2)}) copy-start(s32[1024]{0:T(1024)} %param.13) | copy-start | bytes 12292
  1.4 0.7 %copy-start.5 = (s32[1024]{0:T(1024)S(1)}, s32[1024]{0:T(1024)}, u32[]{:S(2)}) copy-start(s32[1024]{0:T(1024)} %param.12) | copy-start | bytes 12292
  3.4 26.0 %all-to-all-start = ((s32[128,1,1152]{2,1,0:T(1,128)}), s32[128,1,1152]{2,1,0:T(1,128)S(1)}, u32[]{:S(2)}, u32[]{:S(2)}) async-start(s32[128,1,1152]{2,1,0:T(1,128)} %shard_map.83), calls=%async_computation | async-start | bytes 1179648 | tf_op jit(solution)/shard_map/all_to_all | solution.py:209
  14.9 2.2 %copy-start = (bf16[64,32768]{1,0:T(8,128)(2,1)S(1)}, bf16[64,32768]{1,0:T(8,128)(2,1)}, u32[]{:S(2)}) copy-start(bf16[64,32768]{1,0:T(8,128)(2,1)} %dos_ref.1) | copy-start | bytes 12582916
  17.1 1.0 %copy-start.3 = (bf16[1024,256]{1,0:T(8,128)(2,1)S(1)}, bf16[1024,256]{1,0:T(8,128)(2,1)}, u32[]{:S(2)}) copy-start(bf16[1024,256]{1,0:T(8,128)(2,1)} %proj_ref.1) | copy-start | bytes 1572868
  18.1 0.7 %copy-start.6 = (s32[1024]{0:T(1024)S(1)}, s32[1024]{0:T(1024)}, u32[]{:S(2)}) copy-start(s32[1024]{0:T(1024)} %param.9) | copy-start | bytes 12292
  18.8 0.7 %copy-start.7 = (f32[1024]{0:T(1024)S(1)}, f32[1024]{0:T(1024)}, u32[]{:S(2)}) copy-start(f32[1024]{0:T(1024)} %param.10) | copy-start | bytes 12292
  19.5 0.7 %copy-start.8 = (f32[1024]{0:T(1024)S(1)}, f32[1024]{0:T(1024)}, u32[]{:S(2)}) copy-start(f32[1024]{0:T(1024)} %param.11) | copy-start | bytes 12292
  23.4 2.0 %copy-start.1 = (bf16[32,64,1024]{2,1,0:T(8,128)(2,1)}, bf16[32,64,1024]{2,1,0:T(8,128)(2,1)S(1)}, u32[]{:S(2)}) copy-start(bf16[32,64,1024]{2,1,0:T(8,128)(2,1)S(1)} %get-tuple-element.9.xs_ref) | copy-start | bytes 12582916
  29.4 2.2 %copy-start.2 = (bf16[32,64,1024]{2,1,0:T(8,128)(2,1)S(1)}, bf16[32,64,1024]{2,1,0:T(8,128)(2,1)}, u32[]{:S(2)}) copy-start(bf16[32,64,1024]{2,1,0:T(8,128)(2,1)} %copy-done.1) | copy-start | bytes 12582916

commit v3 on v2

v3 whole, which is shorter than its diff:
```python
import math

import jax
import jax.numpy as jnp
from jax import lax
from jax.experimental import pallas as pl
from jax.experimental.pallas import tpu as pltpu
from jax.sharding import PartitionSpec as P

V = 1024
K = 256
SECTION = 1024
LOW = 256
HIGH = SECTION // LOW
CAP = 64
LANES = 128
UNROLL1, UNROLL2, UNROLL3, UNROLL4 = 8, 1, 8, 8
BF = jnp.bfloat16
F32 = jnp.float32
NT = (((1,), (1,)), ((), ()))
TN = (((0,), (0,)), ((), ()))


def iota(shape, axis):
    return lax.broadcasted_iota(jnp.int32, shape, axis)


def small(ints):
    return ints.astype(F32).astype(BF)


def copy_in(pairs, sem):
    copies = [pltpu.make_async_copy(src, dst, sem.at[i]) for i, (src, dst) in enumerate(pairs)]
    for c in copies:
        c.start()
    return copies


def invert_kernel(place_ref, perm_hbm, sign_hbm, rows_hbm, out_hbm, perm_ref, sign_ref, rows_ref, send_ref, sem):
    for c in copy_in(((perm_hbm, perm_ref), (sign_hbm, sign_ref), (rows_hbm, rows_ref)), sem):
        c.wait()
    spot = perm_ref[...] & (SECTION - 1)
    group_of = SECTION // LANES
    row = iota((2 * group_of, SECTION), 0)
    position = iota((2 * group_of, SECTION), 1)
    negative = (sign_ref[...] < 0).astype(jnp.int32)
    digit = jnp.where(row < group_of, position % LANES, position // LANES + group_of * negative)
    digit = jnp.where(spot // LANES == row % group_of, digit, 0)
    hot = jnp.where(small(spot % LANES) == small(iota((LANES, SECTION), 0)), jnp.array(1, BF), jnp.array(0, BF))
    found = lax.dot_general(small(digit), hot, NT, preferred_element_type=F32).astype(jnp.int32)
    code = found[:group_of] + LANES * found[group_of:]
    rows = jnp.concatenate([rows_ref[...] & (SECTION - 1)] * 4, axis=1)
    mine = jnp.where(iota((1, LANES), 1) // 32 == place_ref[0], rows, 0)
    count = send_ref.shape[0]
    for h in range(group_of):
        send_ref[:, :, h * LANES : (h + 1) * LANES] = jnp.broadcast_to(code[h : h + 1][None], (count, 1, LANES))
    send_ref[:, :, SECTION:] = jnp.broadcast_to(mine[None], (count, 1, LANES))
    total = out_hbm.shape[0] // count
    copies = copy_in([(send_ref, out_hbm.at[pl.ds(i * count, count)]) for i in range(total)], sem)
    for c in copies:
        c.wait()


def ready_kernel(
    place_ref, dos_hbm, slot_hbm, cen_hbm, scl_hbm, proj_hbm, out_hbm, gain_ref, had_ref, sp_ref,
    dos, xs, slot_ref, cen_ref, scl_ref, proj_ref, sem,
):
    chunks = dos.shape[0]
    per = xs.shape[1]
    width = per * SECTION
    pairs = [(slot_hbm, slot_ref), (cen_hbm, cen_ref), (scl_hbm, scl_ref)]
    pairs += [(dos_hbm.at[:, pl.ds(c * width, width)], dos.at[c]) for c in range(chunks)]
    copies = copy_in(pairs + [(proj_hbm, proj_ref)], sem)
    bits = iota((LOW, LOW), 0) & iota((LOW, LOW), 1)
    bits = bits ^ (bits >> 4)
    bits = bits ^ (bits >> 2)
    bits = bits ^ (bits >> 1)
    had_ref[...] = small(1 - 2 * (bits & 1))
    for c in copies[:3]:
        c.wait()
    mine = jnp.broadcast_to(slot_ref[...], (CAP, V)) == iota((CAP, V), 0) + place_ref[0] * CAP
    center = jnp.sum(jnp.where(mine, jnp.broadcast_to(cen_ref[...], (CAP, V)), 0.0), axis=1, keepdims=True)
    scale = jnp.sum(jnp.where(mine, jnp.broadcast_to(scl_ref[...], (CAP, V)), 0.0), axis=1, keepdims=True)
    gain_ref[...] = jnp.broadcast_to(scale, (CAP, LANES))
    sends = []
    for c in range(chunks):
        copies[3 + c].wait()
        for i in range(per):
            xs[c, i] = (dos[c, :, i * SECTION : (i + 1) * SECTION].astype(F32) - center).astype(BF)
        sends.append(pltpu.make_async_copy(xs.at[c], out_hbm.at[pl.ds(c * per, per)], sem.at[c]))
        sends[-1].start()
    copies[-1].wait()

    slot = slot_ref[...]
    target = (slot // 16 % 4) * 512 + slot // CAP * 16 + slot % 16
    rows = 256
    for c in range(sp_ref.shape[0] // rows):
        hot = (jnp.broadcast_to(target, (rows, V)) == iota((rows, V), 0) + c * rows).astype(F32).astype(BF)
        sp_ref[c * rows : (c + 1) * rows] = jnp.dot(hot, proj_ref[...], preferred_element_type=F32).astype(BF)
    for c in sends:
        c.wait()


def mix_kernel(place_ref, xs_hbm, got_ref, gain_ref, had_ref, out_ref, xs_ref, spots, mix, tables, sem):
    blocks = xs_ref.shape[0]
    group = place_ref[0]

    def fetch(b):
        return pltpu.make_async_copy(xs_hbm.at[b], xs_ref.at[b], sem.at[b])

    for b in range(blocks):
        fetch(b).start()
    norm = 1.0 / math.sqrt(SECTION * blocks * 4)
    one, zero = jnp.array(1, BF), jnp.array(0, BF)

    def table(i, carry):
        row = jnp.concatenate([sum(got_ref[g * blocks + 2 * i + u, :, SECTION:] for g in range(4)) for u in range(2)], axis=1)
        hot = jnp.where(jnp.broadcast_to(small(row & (LOW - 1)), (LOW, 2 * LANES)) == small(iota((LOW, 2 * LANES), 0)), one, zero)
        both = jnp.dot(had_ref[...], hot, preferred_element_type=F32).astype(BF)
        tables[2 * i] = both[:, :LANES]
        tables[2 * i + 1] = both[:, LANES:]
        return carry

    lax.fori_loop(0, blocks // 2, table, 0, unroll=UNROLL4)

    def place(i, carry):
        for u in range(UNROLL1):
            fetch(i * UNROLL1 + u).wait()
        for u in range(UNROLL1):
            b = i * UNROLL1 + u
            code = got_ref[group * blocks + b, :, 0:SECTION]
            low = jnp.broadcast_to(small(code & (LOW - 1)), (LOW, SECTION))
            flip = jnp.broadcast_to(small(1 - 2 * (code // SECTION)), (LOW, SECTION))
            high = jnp.broadcast_to(small((code // LOW) & (HIGH - 1)), (CAP, SECTION))
            shifted = xs_ref[b]
            parts = [jnp.where(high == jnp.array(h, BF), shifted, zero) for h in range(HIGH)]
            hot = jnp.where(low == small(iota((LOW, SECTION), 0)), flip, zero)
            spot = lax.dot_general(jnp.concatenate(parts, axis=0), hot, NT, preferred_element_type=F32)
            spots[b] = spot.reshape(spots.shape[1:])
        return carry

    lax.fori_loop(0, blocks // UNROLL1, place, 0)

    def cross(i, carry):
        cols = pl.ds(pl.multiple_of(i % (LOW // LANES) * LANES, LANES), LANES)
        i = i // (LOW // LANES)
        vals = [spots[b, i, :, cols].astype(BF) for b in range(blocks)]
        step = 1
        while step < blocks:
            nxt = list(vals)
            for b in range(blocks):
                if not b & step:
                    nxt[b] = vals[b] + vals[b + step]
                    nxt[b + step] = vals[b] - vals[b + step]
            vals = nxt
            step *= 2
        for b in range(blocks):
            mix[b, i, :, cols] = vals[b]
        return carry

    lax.fori_loop(0, mix.shape[1] * (LOW // LANES), cross, 0, unroll=UNROLL2)

    lane = iota((16, LANES), 1) // 32
    gain = gain_ref[...] * norm

    def sample(d, carry):
        raw = jnp.dot(mix[d].reshape(HIGH * CAP, LOW), tables[d], preferred_element_type=F32)
        parts = [raw[h * CAP : (h + 1) * CAP] for h in range(HIGH)]
        top = sum(got_ref[g * blocks + d, :, SECTION:] for g in range(4)) // LOW
        while len(parts) > 1:
            sign = (1 - 2 * (top & 1)).astype(F32)
            parts = [parts[i] + sign * parts[i + 1] for i in range(0, len(parts), 2)]
            top = top // 2
        w = parts[0] * gain
        spun = [w[16 * q : 16 * q + 16] for q in range(4)]
        spun = [spun[0]] + [pltpu.roll(spun[q], 32 * q, 1) for q in range(1, 4)]
        for g in range(4):
            out = spun[0]
            for q in range(1, 4):
                out = jnp.where(lane == (g + q) % 4, spun[q], out)
            out_ref[g, d] = out.astype(BF)
        return carry

    lax.fori_loop(0, blocks, sample, 0, unroll=UNROLL3)


def finish_kernel(place_ref, got_ref, proj_ref, out_ref):
    files = got_ref.shape[1]
    group = place_ref[0]
    odd1 = (1 - 2 * (group % 2)).astype(F32)
    odd2 = (1 - 2 * (group // 2)).astype(F32)
    g = [got_ref[i].astype(F32) for i in range(4)]
    total = (g[0] + odd1 * g[1]) + odd2 * (g[2] + odd1 * g[3])
    total = total.reshape(files * 16, 128).astype(BF)
    out = None
    for q in range(4):
        full = lax.dot_general(total, proj_ref[(q + 4 - group) % 4], TN, preferred_element_type=F32)
        part = full[32 * q : 32 * q + 32]
        out = part if out is None else out + part
    out_ref[...] = out


def vmem(n):
    return [pl.BlockSpec(memory_space=pltpu.VMEM)] * n


def limit(mib):
    return pltpu.CompilerParams(vmem_limit_bytes=mib << 20)


def hbm(n):
    return [pl.BlockSpec(memory_space=pltpu.HBM)] * n


def stay(*arrays):
    return [pltpu.with_memory_space_constraint(a, pltpu.HBM) for a in arrays]


def smem():
    return pl.BlockSpec(memory_space=pltpu.SMEM)


def on_device(
    dosage, variant_slot, center, variant_scale, sample_signs, sample_perm, sample_rows, projection
):
    groups, devs = lax.axis_size("grp"), lax.axis_size("dev")
    both = ("grp", "dev")
    group, dev = lax.axis_index("grp"), lax.axis_index("dev")
    send = pl.pallas_call(
        invert_kernel,
        out_shape=jax.ShapeDtypeStruct((groups * devs, 1, SECTION + LANES), jnp.int32),
        in_specs=[smem()] + hbm(3),
        out_specs=hbm(1)[0],
        scratch_shapes=[
            pltpu.VMEM((1, SECTION), jnp.int32),
            pltpu.VMEM((1, SECTION), jnp.int32),
            pltpu.VMEM((1, 32), jnp.int32),
            pltpu.VMEM((8, 1, SECTION + LANES), jnp.int32),
            pltpu.SemaphoreType.DMA((groups * devs // 8,)),
        ],
        compiler_params=limit(8),
    )(group[None], *stay(sample_perm[None], sample_signs[None], sample_rows[None]))
    chunks = 8
    per = devs // chunks
    xs, gain, had, slot_proj = pl.pallas_call(
        ready_kernel,
        out_shape=(
            pltpu.HBM((devs, CAP, SECTION), BF),
            jax.ShapeDtypeStruct((CAP, LANES), F32),
            jax.ShapeDtypeStruct((LOW, LOW), BF),
            jax.ShapeDtypeStruct((devs * CAP, K), BF),
        ),
        in_specs=[smem()] + hbm(5),
        out_specs=tuple(hbm(1) + vmem(3)),
        scratch_shapes=[
            pltpu.VMEM((chunks, CAP, per * SECTION), BF),
            pltpu.VMEM((chunks, per, CAP, SECTION), BF),
            pltpu.VMEM((1, V), jnp.int32),
            pltpu.VMEM((1, V), F32),
            pltpu.VMEM((1, V), F32),
            pltpu.VMEM((V, K), BF),
            pltpu.SemaphoreType.DMA((chunks + 4,)),
        ],
        compiler_params=limit(16),
    )(dev[None], *stay(dosage, variant_slot[None], center[None], variant_scale[None], projection))
    got = lax.all_to_all(send, both, 0, 0, tiled=True)
    mixed = pl.pallas_call(
        mix_kernel,
        out_shape=jax.ShapeDtypeStruct((groups, devs, 16, LANES), BF),
        in_specs=[smem()] + hbm(1) + vmem(3),
        out_specs=pl.BlockSpec(memory_space=pltpu.VMEM),
        compiler_params=limit(32),
        scratch_shapes=[
            pltpu.VMEM((devs, CAP, SECTION), BF),
            pltpu.VMEM((devs, HIGH * CAP // 16, 16, LOW), F32),
            pltpu.VMEM((devs, HIGH * CAP // 16, 16, LOW), BF),
            pltpu.VMEM((devs, LOW, LANES), BF),
            pltpu.SemaphoreType.DMA((devs,)),
        ],
    )(group[None], *stay(xs), got, gain, had)
    mixed = mixed.reshape(groups * devs, 16, 128)
    got = lax.all_to_all(mixed, both, 0, 0, tiled=True).reshape(groups, devs, 16, 128)
    return pl.pallas_call(
        finish_kernel,
        out_shape=jax.ShapeDtypeStruct((32, K), F32),
        in_specs=[smem()] + vmem(2),
        out_specs=pl.BlockSpec(memory_space=pltpu.VMEM),
        compiler_params=limit(8),
    )(group[None], got, slot_proj.reshape(4, devs * 16, K))


def solution(mesh):
    return jax.shard_map(
        on_device,
        mesh=mesh,
        in_specs=(
            P("dev", "grp"),
            P(),
            P(),
            P(),
            P(("grp", "dev")),
            P(("grp", "dev")),
            P(("grp", "dev")),
            P(),
        ),
        out_specs=P(("grp", "dev"), None),
        check_vma=False,
    )
```

time: 68 us -> 57.7 us (0.85)
  local copies, waits for them, and re-layouts: 11.5 us -> 0 us
  waiting for transfers between devices: 4.08 us -> 10.1 us
  Pallas kernels: 21.1 us -> 17.9 us
  blocking collectives: 19.3 us -> 18 us
    unnamed x18 -> x0, local copies, waits for them, and re-layouts: 10.8 us -> none
    all_to_all x1, waiting for transfers between devices: 4.08 us -> 10.1 us  [on_device(): got = lax.all_to_all(send, both, 0, 0, tiled=True)]
    pallas_call x1, Pallas kernels: 15.6 us -> 10.6 us  [on_device(): pl.pallas_call(mix_kernel, out_shape=jax.ShapeDtypeStruct((groups, devs,...]
    all_to_all x1, blocking collectives: 19.3 us -> 18 us  [on_device(): lax.all_to_all(mixed, both, 0, 0, tiled=True).reshape(groups, devs, 16, 128)]
    pallas_call x1, Pallas kernels: 3.19 us -> 4.41 us  [on_device(): pl.pallas_call(ready_kernel, out_shape=(pltpu.HBM((devs, CAP, SECTION), B...]
    another operation x2 -> x0, local copies, waits for them, and re-layouts: 0.74 us -> none  [on_device(): jnp.tile(sample_rows, 4)[None]]
  transfers between devices with their start and end apart: 1 -> 1, of which waited for: 1 -> 1; matrix products, arithmetic and copies ran while one was open for 0% -> 0% of each run, Pallas kernels for 5% -> 8%
where the time goes in v3:
time: 57.7 us; the launch traced here: 57.5 us
  blocking collectives  18 us (31%)
  Pallas kernels  17.9 us (31%)
  starting transfers between devices  11.5 us (20%)
  waiting for transfers between devices  10.1 us (18%)
    all_to_all x1, blocking collectives, on_device(): lax.all_to_all(mixed, both, 0, 0, tiled=True).reshape(groups, devs, 16, 128)  18 us
    all_to_all x1, starting transfers between devices, on_device(): got = lax.all_to_all(send, both, 0, 0, tiled=True)  11.5 us
    pallas_call x1, Pallas kernels, on_device(): pl.pallas_call(mix_kernel, out_shape=jax.ShapeDtypeStruct((groups, devs,...  10.6 us
    all_to_all x1, waiting for transfers between devices, on_device(): got = lax.all_to_all(send, both, 0, 0, tiled=True)  10.1 us
    pallas_call x1, Pallas kernels, on_device(): pl.pallas_call(ready_kernel, out_shape=(pltpu.HBM((devs, CAP, SECTION), B...  4.41 us
    pallas_call x1, Pallas kernels, on_device(): pl.pallas_call(invert_kernel, out_shape=jax.ShapeDtypeStruct((groups * de...  1.89 us
  transfers between devices with their start and end apart: 1, of which 1 were waited for; matrix products, arithmetic and copies ran while one was open for 0% of the time, Pallas kernels for 8%

profile of v3, /device:TPU:1, one launch (start us, length us, event | category | flops | bytes accessed | tf_op | source)
XLA Modules:
  0.0 57.5 jit_solution(11932635500764631845)
XLA Ops:
  0.0 1.9 %shard_map.83 = s32[128,1,1152]{2,1,0:T(1,128)} custom-call(s32[1]{0:T(128)} %bitcast.place_ref, s32[1,1024]{1,0:T(1,128)} %bitcast.14, s32[1,1024]{1,0:T(1,128)} %bitcast.15, s32[1,32]{1,0:T(1,128)} %bitcast.19), custom_call_target="tpu_custom_call" | custom-call | tf_op jit(solution)/shard_map/pallas_call | solution.py:229
  1.9 11.5 %all-to-all-start = ((s32[128,1,1152]{2,1,0:T(1,128)}), s32[128,1,1152]{2,1,0:T(1,128)S(1)}, u32[]{:S(2)}, u32[]{:S(2)}) async-start(s32[128,1,1152]{2,1,0:T(1,128)} %shard_map.83), calls=%async_computation | async-start | bytes 1179648 | tf_op jit(solution)/shard_map/all_to_all | solution.py:266
  13.4 4.4 %shard_map.82 = (bf16[32,64,1024]{2,1,0:T(8,128)(2,1)}, f32[64,128]{1,0:T(8,128)S(1)}, bf16[256,256]{1,0:T(8,128)(2,1)S(1)}, bf16[2048,256]{1,0:T(8,128)(2,1)S(1)}) custom-call(s32[1]{0:T(128)} %bitcast.1.place_ref, bf16[64,32768]{1,0:T(8,128)(2,1)} %dos_hbm.1, s32[1,1024]{1,0:T(1,128)} %bitcast.16, f32[1,1024]{1,0:T(1,128)} %bitcast.17, ...), custom_call_target="tpu_custom_call" | custom-call | tf_op jit(solution)/shard_map/pallas_call | solution.py:245
  17.8 10.1 %all-to-all-done.got_ref = s32[128,1,1152]{2,1,0:T(1,128)S(1)} async-done(((s32[128,1,1152]{2,1,0:T(1,128)}), s32[128,1,1152]{2,1,0:T(1,128)S(1)}, u32[]{:S(2)}, u32[]{:S(2)}) %all-to-all-start) | async-done | bytes 589856 | tf_op jit(solution)/shard_map/all_to_all | solution.py:266
  27.9 10.6 %shard_map.84 = bf16[4,32,16,128]{3,2,1,0:T(8,128)(2,1)S(1)} custom-call(s32[1]{0:T(128)} %bitcast.place_ref, bf16[32,64,1024]{2,1,0:T(8,128)(2,1)} %get-tuple-element.9.xs_hbm, s32[128,1,1152]{2,1,0:T(1,128)S(1)} %all-to-all-done.got_ref, f32[64,128]{1,0:T(8,128)S(1)} %get-tuple-element.10.gain_ref, bf16[256,256]{1,0:T(8,128)(2,1)S(1)} %get-tuple-element.11.had_ref), custom_call_target="tpu_custom_call" | custom-call | tf_op jit(solution)/shard_map/pallas_call | solution.py:267
  38.5 18.0 %all_to_all.10 = bf16[128,16,128]{2,1,0:T(8,128)(2,1)S(1)} all-to-all(bf16[128,16,128]{2,1,0:T(8,128)(2,1)S(1)} %bitcast.12), channel_id=1, replica_groups=mesh['grp'=4,'dev'=32] {'grp','dev'}, dimensions={0} | all-to-all | bytes 1048576 | tf_op jit(solution)/shard_map/all_to_all | solution.py:282
  56.5 1.0 %shard_map.85 = f32[32,256]{1,0:T(8,128)} custom-call(s32[1]{0:T(128)} %bitcast.place_ref, bf16[4,32,16,128]{3,2,1,0:T(8,128)(2,1)S(1)} %bitcast.11, bf16[4,512,256]{2,1,0:T(8,128)(2,1)S(1)} %bitcast.13), custom_call_target="tpu_custom_call" | custom-call | tf_op jit(solution)/shard_map/pallas_call | solution.py:283
Async XLA Ops:
  1.9 26.0 %all-to-all-start = ((s32[128,1,1152]{2,1,0:T(1,128)}), s32[128,1,1152]{2,1,0:T(1,128)S(1)}, u32[]{:S(2)}, u32[]{:S(2)}) async-start(s32[128,1,1152]{2,1,0:T(1,128)} %shard_map.83), calls=%async_computation | async-start | bytes 1179648 | tf_op jit(solution)/shard_map/all_to_all | solution.py:266

commit v4 on v3

--- a/solution.py
+++ b/solution.py
@@ -14,7 +14,7 @@
 HIGH = SECTION // LOW
 CAP = 64
 LANES = 128
-UNROLL1, UNROLL2, UNROLL3, UNROLL4 = 8, 1, 8, 8
+UNROLL1, UNROLL2, UNROLL3, UNROLL4, FUSED = 16, 64, 16, 8, 4
 BF = jnp.bfloat16
 F32 = jnp.float32
 NT = (((1,), (1,)), ((), ()))
@@ -101,7 +101,15 @@
         c.wait()
 
 
-def mix_kernel(place_ref, xs_hbm, got_ref, gain_ref, had_ref, out_ref, xs_ref, spots, mix, tables, sem):
+def butterflies(vals, step):
+    while step < len(vals):
+        pairs = {b: (vals[b] + vals[b + step], vals[b] - vals[b + step]) for b in range(len(vals)) if not b & step}
+        vals = [pairs[b & ~step][1 if b & step else 0] for b in range(len(vals))]
+        step *= 2
+    return vals
+
+
+def mix_kernel(place_ref, xs_hbm, got_ref, gain_ref, had_ref, out_ref, xs_ref, spots, tables, sem):
     blocks = xs_ref.shape[0]
     group = place_ref[0]
 
@@ -126,6 +134,7 @@
     def place(i, carry):
         for u in range(UNROLL1):
             fetch(i * UNROLL1 + u).wait()
+        held = []
         for u in range(UNROLL1):
             b = i * UNROLL1 + u
             code = got_ref[group * blocks + b, :, 0:SECTION]
@@ -136,35 +145,31 @@
             parts = [jnp.where(high == jnp.array(h, BF), shifted, zero) for h in range(HIGH)]
             hot = jnp.where(low == small(iota((LOW, SECTION), 0)), flip, zero)
             spot = lax.dot_general(jnp.concatenate(parts, axis=0), hot, NT, preferred_element_type=F32)
-            spots[b] = spot.reshape(spots.shape[1:])
+            held.append(spot)
+            if len(held) == FUSED:
+                held = butterflies(held, 1)
+                for v in range(FUSED):
+                    spots[b - FUSED + 1 + v] = held[v]
+                held = []
         return carry
 
     lax.fori_loop(0, blocks // UNROLL1, place, 0)
 
     def cross(i, carry):
+        rows = pl.ds(pl.multiple_of(i // (LOW // LANES) * 8, 8), 8)
         cols = pl.ds(pl.multiple_of(i % (LOW // LANES) * LANES, LANES), LANES)
-        i = i // (LOW // LANES)
-        vals = [spots[b, i, :, cols].astype(BF) for b in range(blocks)]
-        step = 1
-        while step < blocks:
-            nxt = list(vals)
-            for b in range(blocks):
-                if not b & step:
-                    nxt[b] = vals[b] + vals[b + step]
-                    nxt[b + step] = vals[b] - vals[b + step]
-            vals = nxt
-            step *= 2
+        vals = butterflies([spots[b, rows, cols] for b in range(blocks)], FUSED)
         for b in range(blocks):
-            mix[b, i, :, cols] = vals[b]
+            spots[b, rows, cols] = vals[b]
         return carry
 
-    lax.fori_loop(0, mix.shape[1] * (LOW // LANES), cross, 0, unroll=UNROLL2)
+    lax.fori_loop(0, HIGH * CAP // 8 * (LOW // LANES), cross, 0, unroll=UNROLL2)
 
     lane = iota((16, LANES), 1) // 32
     gain = gain_ref[...] * norm
 
     def sample(d, carry):
-        raw = jnp.dot(mix[d].reshape(HIGH * CAP, LOW), tables[d], preferred_element_type=F32)
+        raw = jnp.dot(spots[d].astype(BF), tables[d], preferred_element_type=F32)
         parts = [raw[h * CAP : (h + 1) * CAP] for h in range(HIGH)]
         top = sum(got_ref[g * blocks + d, :, SECTION:] for g in range(4)) // LOW
         while len(parts) > 1:
@@ -272,8 +277,7 @@
         compiler_params=limit(32),
         scratch_shapes=[
             pltpu.VMEM((devs, CAP, SECTION), BF),
-            pltpu.VMEM((devs, HIGH * CAP // 16, 16, LOW), F32),
-            pltpu.VMEM((devs, HIGH * CAP // 16, 16, LOW), BF),
+            pltpu.VMEM((devs, HIGH * CAP, LOW), F32),
             pltpu.VMEM((devs, LOW, LANES), BF),
             pltpu.SemaphoreType.DMA((devs,)),
         ],

time: 57.7 us -> 56.7 us (0.983)
  Pallas kernels: 17.9 us -> 16.9 us
    pallas_call x1, Pallas kernels: 10.6 us -> 9.58 us  [on_device(): pl.pallas_call(mix_kernel, out_shape=jax.ShapeDtypeStruct((groups, devs,...]
where the time goes in v4:
time: 56.7 us; the launch traced here: 56.5 us
  blocking collectives  18 us (32%)
  Pallas kernels  16.9 us (30%)
  starting transfers between devices  11.5 us (20%)
  waiting for transfers between devices  10.1 us (18%)
    all_to_all x1, blocking collectives, on_device(): lax.all_to_all(mixed, both, 0, 0, tiled=True).reshape(groups, devs, 16, 128)  18 us
    all_to_all x1, starting transfers between devices, on_device(): got = lax.all_to_all(send, both, 0, 0, tiled=True)  11.5 us
    all_to_all x1, waiting for transfers between devices, on_device(): got = lax.all_to_all(send, both, 0, 0, tiled=True)  10.1 us
    pallas_call x1, Pallas kernels, on_device(): pl.pallas_call(mix_kernel, out_shape=jax.ShapeDtypeStruct((groups, devs,...  9.58 us
    pallas_call x1, Pallas kernels, on_device(): pl.pallas_call(ready_kernel, out_shape=(pltpu.HBM((devs, CAP, SECTION), B...  4.41 us
    pallas_call x1, Pallas kernels, on_device(): pl.pallas_call(invert_kernel, out_shape=jax.ShapeDtypeStruct((groups * de...  1.89 us
  transfers between devices with their start and end apart: 1, of which 1 were waited for; matrix products, arithmetic and copies ran while one was open for 0% of the time, Pallas kernels for 8%

profile of v4, /device:TPU:1, one launch (start us, length us, event | category | flops | bytes accessed | tf_op | source)
XLA Modules:
  0.0 56.5 jit_solution(6124872275054850645)
XLA Ops:
  0.0 1.9 %shard_map.83 = s32[128,1,1152]{2,1,0:T(1,128)} custom-call(s32[1]{0:T(128)} %bitcast.place_ref, s32[1,1024]{1,0:T(1,128)} %bitcast.14, s32[1,1024]{1,0:T(1,128)} %bitcast.15, s32[1,32]{1,0:T(1,128)} %bitcast.19), custom_call_target="tpu_custom_call" | custom-call | tf_op jit(solution)/shard_map/pallas_call | solution.py:234
  1.9 11.5 %all-to-all-start = ((s32[128,1,1152]{2,1,0:T(1,128)}), s32[128,1,1152]{2,1,0:T(1,128)S(1)}, u32[]{:S(2)}, u32[]{:S(2)}) async-start(s32[128,1,1152]{2,1,0:T(1,128)} %shard_map.83), calls=%async_computation | async-start | bytes 1179648 | tf_op jit(solution)/shard_map/all_to_all | solution.py:271
  13.4 4.4 %shard_map.82 = (bf16[32,64,1024]{2,1,0:T(8,128)(2,1)}, f32[64,128]{1,0:T(8,128)S(1)}, bf16[256,256]{1,0:T(8,128)(2,1)S(1)}, bf16[2048,256]{1,0:T(8,128)(2,1)S(1)}) custom-call(s32[1]{0:T(128)} %bitcast.1.place_ref, bf16[64,32768]{1,0:T(8,128)(2,1)} %dos_hbm.1, s32[1,1024]{1,0:T(1,128)} %bitcast.16, f32[1,1024]{1,0:T(1,128)} %bitcast.17, ...), custom_call_target="tpu_custom_call" | custom-call | tf_op jit(solution)/shard_map/pallas_call | solution.py:250
  17.8 10.1 %all-to-all-done.got_ref = s32[128,1,1152]{2,1,0:T(1,128)S(1)} async-done(((s32[128,1,1152]{2,1,0:T(1,128)}), s32[128,1,1152]{2,1,0:T(1,128)S(1)}, u32[]{:S(2)}, u32[]{:S(2)}) %all-to-all-start) | async-done | bytes 589856 | tf_op jit(solution)/shard_map/all_to_all | solution.py:271
  27.9 9.6 %shard_map.84 = bf16[4,32,16,128]{3,2,1,0:T(8,128)(2,1)S(1)} custom-call(s32[1]{0:T(128)} %bitcast.place_ref, bf16[32,64,1024]{2,1,0:T(8,128)(2,1)} %get-tuple-element.9.xs_hbm, s32[128,1,1152]{2,1,0:T(1,128)S(1)} %all-to-all-done.got_ref, f32[64,128]{1,0:T(8,128)S(1)} %get-tuple-element.10.gain_ref, bf16[256,256]{1,0:T(8,128)(2,1)S(1)} %get-tuple-element.11.had_ref), custom_call_target="tpu_custom_call" | custom-call | tf_op jit(solution)/shard_map/pallas_call | solution.py:272
  37.5 18.0 %all_to_all.10 = bf16[128,16,128]{2,1,0:T(8,128)(2,1)S(1)} all-to-all(bf16[128,16,128]{2,1,0:T(8,128)(2,1)S(1)} %bitcast.12), channel_id=1, replica_groups=mesh['grp'=4,'dev'=32] {'grp','dev'}, dimensions={0} | all-to-all | bytes 1048576 | tf_op jit(solution)/shard_map/all_to_all | solution.py:286
  55.5 1.0 %shard_map.85 = f32[32,256]{1,0:T(8,128)} custom-call(s32[1]{0:T(128)} %bitcast.place_ref, bf16[4,32,16,128]{3,2,1,0:T(8,128)(2,1)S(1)} %bitcast.11, bf16[4,512,256]{2,1,0:T(8,128)(2,1)S(1)} %bitcast.13), custom_call_target="tpu_custom_call" | custom-call | tf_op jit(solution)/shard_map/pallas_call | solution.py:287
Async XLA Ops:
  1.9 26.0 %all-to-all-start = ((s32[128,1,1152]{2,1,0:T(1,128)}), s32[128,1,1152]{2,1,0:T(1,128)S(1)}, u32[]{:S(2)}, u32[]{:S(2)}) async-start(s32[128,1,1152]{2,1,0:T(1,128)} %shard_map.83), calls=%async_computation | async-start | bytes 1179648 | tf_op jit(solution)/shard_map/all_to_all | solution.py:271

commit v5 on v4

--- a/solution.py
+++ b/solution.py
@@ -14,7 +14,7 @@
 HIGH = SECTION // LOW
 CAP = 64
 LANES = 128
-UNROLL1, UNROLL2, UNROLL3, UNROLL4, FUSED = 16, 64, 16, 8, 4
+UNROLL1, UNROLL2, UNROLL3, UNROLL4, FUSED = 16, 64, 32, 8, 4
 BF = jnp.bfloat16
 F32 = jnp.float32
 NT = (((1,), (1,)), ((), ()))
@@ -62,7 +62,7 @@
 
 
 def ready_kernel(
-    place_ref, dos_hbm, slot_hbm, cen_hbm, scl_hbm, proj_hbm, out_hbm, gain_ref, had_ref, sp_ref,
+    place_ref, dos_hbm, slot_hbm, cen_hbm, scl_hbm, proj_hbm, x0, x1, out_hbm, gain_ref, sp_ref,
     dos, xs, slot_ref, cen_ref, scl_ref, proj_ref, sem,
 ):
     chunks = dos.shape[0]
@@ -71,11 +71,6 @@
     pairs = [(slot_hbm, slot_ref), (cen_hbm, cen_ref), (scl_hbm, scl_ref)]
     pairs += [(dos_hbm.at[:, pl.ds(c * width, width)], dos.at[c]) for c in range(chunks)]
     copies = copy_in(pairs + [(proj_hbm, proj_ref)], sem)
-    bits = iota((LOW, LOW), 0) & iota((LOW, LOW), 1)
-    bits = bits ^ (bits >> 4)
-    bits = bits ^ (bits >> 2)
-    bits = bits ^ (bits >> 1)
-    had_ref[...] = small(1 - 2 * (bits & 1))
     for c in copies[:3]:
         c.wait()
     mine = jnp.broadcast_to(slot_ref[...], (CAP, V)) == iota((CAP, V), 0) + place_ref[0] * CAP
@@ -85,18 +80,26 @@
     sends = []
     for c in range(chunks):
         copies[3 + c].wait()
+        half, quarter = divmod(c, 4)
+        spot = 2 * half + quarter - 2
         for i in range(per):
-            xs[c, i] = (dos[c, :, i * SECTION : (i + 1) * SECTION].astype(F32) - center).astype(BF)
-        sends.append(pltpu.make_async_copy(xs.at[c], out_hbm.at[pl.ds(c * per, per)], sem.at[c]))
-        sends[-1].start()
+            shifted = (dos[c, :, i * SECTION : (i + 1) * SECTION].astype(F32) - center).astype(BF)
+            if quarter < 2:
+                (x0, x1)[quarter][half, i] = shifted
+            else:
+                xs[spot, i] = shifted
+        if quarter >= 2:
+            sends.append(pltpu.make_async_copy(xs.at[spot], out_hbm.at[pl.ds(spot * per, per)], sem.at[c]))
+            sends[-1].start()
     copies[-1].wait()
 
     slot = slot_ref[...]
-    target = (slot // 16 % 4) * 512 + slot // CAP * 16 + slot % 16
-    rows = 256
-    for c in range(sp_ref.shape[0] // rows):
-        hot = (jnp.broadcast_to(target, (rows, V)) == iota((rows, V), 0) + c * rows).astype(F32).astype(BF)
-        sp_ref[c * rows : (c + 1) * rows] = jnp.dot(hot, proj_ref[...], preferred_element_type=F32).astype(BF)
+    base = sp_ref.shape[0] - 32
+    target = jnp.where(slot % CAP < 32, (slot // 16 % 2) * (base // 2) + slot // CAP * 16 + slot % 16, base + slot % 32)
+    for start in range(0, sp_ref.shape[0], LOW):
+        rows = min(LOW, sp_ref.shape[0] - start)
+        hot = (jnp.broadcast_to(target, (rows, V)) == iota((rows, V), 0) + start).astype(F32).astype(BF)
+        sp_ref[start : start + rows] = jnp.dot(hot, proj_ref[...], preferred_element_type=F32).astype(BF)
     for c in sends:
         c.wait()
 
@@ -109,31 +112,34 @@
     return vals
 
 
-def mix_kernel(place_ref, xs_hbm, got_ref, gain_ref, had_ref, out_ref, xs_ref, spots, tables, sem):
-    blocks = xs_ref.shape[0]
+def mix_kernel(place_ref, x0, x1, xs_hbm, got_ref, gain_ref, out_ref, xs_ref, spots, sem):
+    blocks = spots.shape[0]
+    far = UNROLL1 // 2
     group = place_ref[0]
 
     def fetch(b):
-        return pltpu.make_async_copy(xs_hbm.at[b], xs_ref.at[b], sem.at[b])
-
-    for b in range(blocks):
+        return pltpu.make_async_copy(xs_hbm.at[pl.ds(b * far, far)], xs_ref.at[pl.ds(b * far, far)], sem.at[b])
+
+    for b in range(blocks // UNROLL1):
         fetch(b).start()
     norm = 1.0 / math.sqrt(SECTION * blocks * 4)
     one, zero = jnp.array(1, BF), jnp.array(0, BF)
 
-    def table(i, carry):
-        row = jnp.concatenate([sum(got_ref[g * blocks + 2 * i + u, :, SECTION:] for g in range(4)) for u in range(2)], axis=1)
-        hot = jnp.where(jnp.broadcast_to(small(row & (LOW - 1)), (LOW, 2 * LANES)) == small(iota((LOW, 2 * LANES), 0)), one, zero)
-        both = jnp.dot(had_ref[...], hot, preferred_element_type=F32).astype(BF)
-        tables[2 * i] = both[:, :LANES]
-        tables[2 * i + 1] = both[:, LANES:]
-        return carry
-
-    lax.fori_loop(0, blocks // 2, table, 0, unroll=UNROLL4)
+    def table(row):
+        def signs(bits):
+            bits = jnp.broadcast_to(bits, (16, LANES)) & iota((16, LANES), 0)
+            bits = bits ^ (bits >> 2)
+            bits = bits ^ (bits >> 1)
+            return (1 - 2 * (bits & 1)).astype(F32)
+
+        upper = signs((row >> 4) & 15)
+        lower = signs(row & 15).astype(BF)
+        return jnp.concatenate(
+            [jnp.broadcast_to(upper[k : k + 1], (16, LANES)).astype(BF) * lower for k in range(16)], axis=0
+        )
 
     def place(i, carry):
-        for u in range(UNROLL1):
-            fetch(i * UNROLL1 + u).wait()
+        fetch(i).wait()
         held = []
         for u in range(UNROLL1):
             b = i * UNROLL1 + u
@@ -141,7 +147,7 @@
             low = jnp.broadcast_to(small(code & (LOW - 1)), (LOW, SECTION))
             flip = jnp.broadcast_to(small(1 - 2 * (code // SECTION)), (LOW, SECTION))
             high = jnp.broadcast_to(small((code // LOW) & (HIGH - 1)), (CAP, SECTION))
-            shifted = xs_ref[b]
+            shifted = (x0, x1)[u // 4][i, u % 4] if u < far else xs_ref[i * far + u - far]
             parts = [jnp.where(high == jnp.array(h, BF), shifted, zero) for h in range(HIGH)]
             hot = jnp.where(low == small(iota((LOW, SECTION), 0)), flip, zero)
             spot = lax.dot_general(jnp.concatenate(parts, axis=0), hot, NT, preferred_element_type=F32)
@@ -169,9 +175,10 @@
     gain = gain_ref[...] * norm
 
     def sample(d, carry):
-        raw = jnp.dot(spots[d].astype(BF), tables[d], preferred_element_type=F32)
+        row = sum(got_ref[g * blocks + d, :, SECTION:] for g in range(4))
+        raw = jnp.dot(spots[d].astype(BF), table(row), preferred_element_type=F32)
         parts = [raw[h * CAP : (h + 1) * CAP] for h in range(HIGH)]
-        top = sum(got_ref[g * blocks + d, :, SECTION:] for g in range(4)) // LOW
+        top = row // LOW
         while len(parts) > 1:
             sign = (1 - 2 * (top & 1)).astype(F32)
             parts = [parts[i] + sign * parts[i + 1] for i in range(0, len(parts), 2)]
@@ -197,10 +204,16 @@
     g = [got_ref[i].astype(F32) for i in range(4)]
     total = (g[0] + odd1 * g[1]) + odd2 * (g[2] + odd1 * g[3])
     total = total.reshape(files * 16, 128).astype(BF)
+    half = files * 16
     out = None
-    for q in range(4):
-        full = lax.dot_general(total, proj_ref[(q + 4 - group) % 4], TN, preferred_element_type=F32)
-        part = full[32 * q : 32 * q + 32]
+    for l in range(4):
+        rows = slice(32 * l, 32 * l + 32)
+        q = (l + 4 - group) % 4
+        low = proj_ref[pl.ds(pl.multiple_of(q % 2 * half, 16), half)]
+        last = proj_ref[pl.ds(pl.multiple_of(2 * half + q % 2 * 16, 16), 16)]
+        first = lax.dot_general(total, low, TN, preferred_element_type=F32)[rows]
+        extra = lax.dot_general(total[half - 16 :], last, TN, preferred_element_type=F32)[rows]
+        part = jnp.where(q < 2, first, extra)
         out = part if out is None else out + part
     out_ref[...] = out
 
@@ -247,19 +260,20 @@
     )(group[None], *stay(sample_perm[None], sample_signs[None], sample_rows[None]))
     chunks = 8
     per = devs // chunks
-    xs, gain, had, slot_proj = pl.pallas_call(
+    x0, x1, xs, gain, slot_proj = pl.pallas_call(
         ready_kernel,
         out_shape=(
-            pltpu.HBM((devs, CAP, SECTION), BF),
+            jax.ShapeDtypeStruct((2, per, CAP, SECTION), BF),
+            jax.ShapeDtypeStruct((2, per, CAP, SECTION), BF),
+            pltpu.HBM((devs // 2, CAP, SECTION), BF),
             jax.ShapeDtypeStruct((CAP, LANES), F32),
-            jax.ShapeDtypeStruct((LOW, LOW), BF),
-            jax.ShapeDtypeStruct((devs * CAP, K), BF),
+            jax.ShapeDtypeStruct((devs * 32 + 32, K), BF),
         ),
         in_specs=[smem()] + hbm(5),
-        out_specs=tuple(hbm(1) + vmem(3)),
+        out_specs=tuple(vmem(2) + hbm(1) + vmem(2)),
         scratch_shapes=[
             pltpu.VMEM((chunks, CAP, per * SECTION), BF),
-            pltpu.VMEM((chunks, per, CAP, SECTION), BF),
+            pltpu.VMEM((chunks // 2, per, CAP, SECTION), BF),
             pltpu.VMEM((1, V), jnp.int32),
             pltpu.VMEM((1, V), F32),
             pltpu.VMEM((1, V), F32),
@@ -272,16 +286,15 @@
     mixed = pl.pallas_call(
         mix_kernel,
         out_shape=jax.ShapeDtypeStruct((groups, devs, 16, LANES), BF),
-        in_specs=[smem()] + hbm(1) + vmem(3),
+        in_specs=[smem()] + vmem(2) + hbm(1) + vmem(2),
         out_specs=pl.BlockSpec(memory_space=pltpu.VMEM),
-        compiler_params=limit(32),
+        compiler_params=limit(24),
         scratch_shapes=[
-            pltpu.VMEM((devs, CAP, SECTION), BF),
+            pltpu.VMEM((devs // 2, CAP, SECTION), BF),
             pltpu.VMEM((devs, HIGH * CAP, LOW), F32),
-            pltpu.VMEM((devs, LOW, LANES), BF),
             pltpu.SemaphoreType.DMA((devs,)),
         ],
-    )(group[None], *stay(xs), got, gain, had)
+    )(group[None], x0, x1, *stay(xs), got, gain)
     mixed = mixed.reshape(groups * devs, 16, 128)
     got = lax.all_to_all(mixed, both, 0, 0, tiled=True).reshape(groups, devs, 16, 128)
     return pl.pallas_call(
@@ -290,7 +303,7 @@
         in_specs=[smem()] + vmem(2),
         out_specs=pl.BlockSpec(memory_space=pltpu.VMEM),
         compiler_params=limit(8),
-    )(group[None], got, slot_proj.reshape(4, devs * 16, K))
+    )(group[None], got, slot_proj)
 
 
 def solution(mesh):

time: 56.7 us -> 56.4 us (level)
  Pallas kernels: 16.9 us -> 15.4 us
  waiting for transfers between devices: 10.1 us -> 11.3 us
    all_to_all x1, waiting for transfers between devices: 10.1 us -> 11.3 us  [on_device(): got = lax.all_to_all(send, both, 0, 0, tiled=True)]
    pallas_call x1, Pallas kernels: 4.41 us -> 3.25 us  [on_device(): pl.pallas_call(ready_kernel, out_shape=(jax.ShapeDtypeStruct((2, per, CAP...]
  transfers between devices with their start and end apart: 1 -> 1, of which waited for: 1 -> 1; matrix products, arithmetic and copies ran while one was open for 0% -> 0% of each run, Pallas kernels for 8% -> 6%
where the time goes in v5:
time: 56.4 us; the launch traced here: 56.2 us
  blocking collectives  18 us (32%)
  Pallas kernels  15.4 us (27%)
  starting transfers between devices  11.5 us (20%)
  waiting for transfers between devices  11.3 us (20%)
    all_to_all x1, blocking collectives, on_device(): lax.all_to_all(mixed, both, 0, 0, tiled=True).reshape(groups, devs, 16, 128)  18 us
    all_to_all x1, starting transfers between devices, on_device(): got = lax.all_to_all(send, both, 0, 0, tiled=True)  11.5 us
    all_to_all x1, waiting for transfers between devices, on_device(): got = lax.all_to_all(send, both, 0, 0, tiled=True)  11.3 us
    pallas_call x1, Pallas kernels, on_device(): pl.pallas_call(mix_kernel, out_shape=jax.ShapeDtypeStruct((groups, devs,...  9.23 us
    pallas_call x1, Pallas kernels, on_device(): pl.pallas_call(ready_kernel, out_shape=(jax.ShapeDtypeStruct((2, per, CAP...  3.25 us
    pallas_call x1, Pallas kernels, on_device(): pl.pallas_call(invert_kernel, out_shape=jax.ShapeDtypeStruct((groups * de...  1.89 us
  transfers between devices with their start and end apart: 1, of which 1 were waited for; matrix products, arithmetic and copies ran while one was open for 0% of the time, Pallas kernels for 6%

profile of v5, /device:TPU:1, one launch (start us, length us, event | category | flops | bytes accessed | tf_op | source)
XLA Modules:
  0.0 56.2 jit_solution(8226287766669925545)
XLA Ops:
  0.0 1.9 %shard_map.83 = s32[128,1,1152]{2,1,0:T(1,128)} custom-call(s32[1]{0:T(128)} %bitcast.place_ref, s32[1,1024]{1,0:T(1,128)} %bitcast.12, s32[1,1024]{1,0:T(1,128)} %bitcast.13, s32[1,32]{1,0:T(1,128)} %bitcast.17), custom_call_target="tpu_custom_call" | custom-call | tf_op jit(solution)/shard_map/pallas_call | solution.py:247
  1.9 11.5 %all-to-all-start = ((s32[128,1,1152]{2,1,0:T(1,128)}), s32[128,1,1152]{2,1,0:T(1,128)S(1)}, u32[]{:S(2)}, u32[]{:S(2)}) async-start(s32[128,1,1152]{2,1,0:T(1,128)} %shard_map.83), calls=%async_computation | async-start | bytes 1179648 | tf_op jit(solution)/shard_map/all_to_all | solution.py:285
  13.4 3.3 %shard_map.82 = (bf16[2,4,64,1024]{3,2,1,0:T(8,128)(2,1)S(1)}, bf16[2,4,64,1024]{3,2,1,0:T(8,128)(2,1)S(1)}, bf16[16,64,1024]{2,1,0:T(8,128)(2,1)}, f32[64,128]{1,0:T(8,128)S(1)}, bf16[1056,256]{1,0:T(8,128)(2,1)S(1)}) custom-call(s32[1]{0:T(128)} %bitcast.1.place_ref, bf16[64,32768]{1,0:T(8,128)(2,1)} %dos_hbm.1, s32[1,1024]{1,0:T(1,128)} %bitcast.14, ...), custom_call_target="tpu_custom_call" | custom-call | tf_op jit(solution)/shard_map/pallas_call | solution.py:263
  16.7 11.3 %all-to-all-done.got_ref = s32[128,1,1152]{2,1,0:T(1,128)S(1)} async-done(((s32[128,1,1152]{2,1,0:T(1,128)}), s32[128,1,1152]{2,1,0:T(1,128)S(1)}, u32[]{:S(2)}, u32[]{:S(2)}) %all-to-all-start) | async-done | bytes 589856 | tf_op jit(solution)/shard_map/all_to_all | solution.py:285
  27.9 9.2 %shard_map.84 = bf16[4,32,16,128]{3,2,1,0:T(8,128)(2,1)S(1)} custom-call(s32[1]{0:T(128)} %bitcast.place_ref, bf16[2,4,64,1024]{3,2,1,0:T(8,128)(2,1)S(1)} %get-tuple-element.10.x0, bf16[2,4,64,1024]{3,2,1,0:T(8,128)(2,1)S(1)} %get-tuple-element.11.x1, bf16[16,64,1024]{2,1,0:T(8,128)(2,1)} %get-tuple-element.12.xs_hbm, ...), custom_call_target="tpu_custom_call" | custom-call | tf_op jit(solution)/shard_map/pallas_call | solution.py:286
  37.2 18.0 %all_to_all.10 = bf16[128,16,128]{2,1,0:T(8,128)(2,1)S(1)} all-to-all(bf16[128,16,128]{2,1,0:T(8,128)(2,1)S(1)} %bitcast.11), channel_id=1, replica_groups=mesh['grp'=4,'dev'=32] {'grp','dev'}, dimensions={0} | all-to-all | bytes 1048576 | tf_op jit(solution)/shard_map/all_to_all | solution.py:299
  55.1 1.0 %shard_map.85 = f32[32,256]{1,0:T(8,128)} custom-call(s32[1]{0:T(128)} %bitcast.place_ref, bf16[4,32,16,128]{3,2,1,0:T(8,128)(2,1)S(1)} %bitcast.10, bf16[1056,256]{1,0:T(8,128)(2,1)S(1)} %get-tuple-element.14.proj_ref), custom_call_target="tpu_custom_call" | custom-call | tf_op jit(solution)/shard_map/pallas_call | solution.py:300
Async XLA Ops:
  1.9 26.0 %all-to-all-start = ((s32[128,1,1152]{2,1,0:T(1,128)}), s32[128,1,1152]{2,1,0:T(1,128)S(1)}, u32[]{:S(2)}, u32[]{:S(2)}) async-start(s32[128,1,1152]{2,1,0:T(1,128)} %shard_map.83), calls=%async_computation | async-start | bytes 1179648 | tf_op jit(solution)/shard_map/all_to_all | solution.py:285

commit v6 on v5

--- a/solution.py
+++ b/solution.py
@@ -196,7 +196,7 @@
     lax.fori_loop(0, blocks, sample, 0, unroll=UNROLL3)
 
 
-def finish_kernel(place_ref, got_ref, proj_ref, out_ref):
+def finish_kernel(place_ref, got_ref, proj_ref, out_ref, full):
     files = got_ref.shape[1]
     group = place_ref[0]
     odd1 = (1 - 2 * (group % 2)).astype(F32)
@@ -205,15 +205,13 @@
     total = (g[0] + odd1 * g[1]) + odd2 * (g[2] + odd1 * g[3])
     total = total.reshape(files * 16, 128).astype(BF)
     half = files * 16
+    for q in range(4):
+        lhs = total if q < 2 else total[half - 16 :]
+        rhs = proj_ref[q * half : (q + 1) * half] if q < 2 else proj_ref[2 * half + (q - 2) * 16 : 2 * half + (q - 1) * 16]
+        full[q] = lax.dot_general(lhs, rhs, TN, preferred_element_type=F32)
     out = None
-    for l in range(4):
-        rows = slice(32 * l, 32 * l + 32)
-        q = (l + 4 - group) % 4
-        low = proj_ref[pl.ds(pl.multiple_of(q % 2 * half, 16), half)]
-        last = proj_ref[pl.ds(pl.multiple_of(2 * half + q % 2 * 16, 16), 16)]
-        first = lax.dot_general(total, low, TN, preferred_element_type=F32)[rows]
-        extra = lax.dot_general(total[half - 16 :], last, TN, preferred_element_type=F32)[rows]
-        part = jnp.where(q < 2, first, extra)
+    for q in range(4):
+        part = full[q, pl.ds(pl.multiple_of((q + group) % 4 * 32, 32), 32)]
         out = part if out is None else out + part
     out_ref[...] = out
 
@@ -253,8 +251,8 @@
             pltpu.VMEM((1, SECTION), jnp.int32),
             pltpu.VMEM((1, SECTION), jnp.int32),
             pltpu.VMEM((1, 32), jnp.int32),
-            pltpu.VMEM((8, 1, SECTION + LANES), jnp.int32),
-            pltpu.SemaphoreType.DMA((groups * devs // 8,)),
+            pltpu.VMEM((16, 1, SECTION + LANES), jnp.int32),
+            pltpu.SemaphoreType.DMA((groups * devs // 16,)),
         ],
         compiler_params=limit(8),
     )(group[None], *stay(sample_perm[None], sample_signs[None], sample_rows[None]))
@@ -302,6 +300,7 @@
         out_shape=jax.ShapeDtypeStruct((32, K), F32),
         in_specs=[smem()] + vmem(2),
         out_specs=pl.BlockSpec(memory_space=pltpu.VMEM),
+        scratch_shapes=[pltpu.VMEM((4, 4 * 32, K), F32)],
         compiler_params=limit(8),
     )(group[None], got, slot_proj)
 

time: 56.4 us -> 56.3 us (level)
  no operation moved by 1% of the time
where the time goes in v6:
time: 56.3 us; the launch traced here: 56 us
  blocking collectives  18 us (32%)
  Pallas kernels  15.3 us (27%)
  starting transfers between devices  11.5 us (20%)
  waiting for transfers between devices  11.3 us (20%)
    all_to_all x1, blocking collectives, on_device(): lax.all_to_all(mixed, both, 0, 0, tiled=True).reshape(groups, devs, 16, 128)  18 us
    all_to_all x1, starting transfers between devices, on_device(): got = lax.all_to_all(send, both, 0, 0, tiled=True)  11.5 us
    all_to_all x1, waiting for transfers between devices, on_device(): got = lax.all_to_all(send, both, 0, 0, tiled=True)  11.3 us
    pallas_call x1, Pallas kernels, on_device(): pl.pallas_call(mix_kernel, out_shape=jax.ShapeDtypeStruct((groups, devs,...  9.22 us
    pallas_call x1, Pallas kernels, on_device(): pl.pallas_call(ready_kernel, out_shape=(jax.ShapeDtypeStruct((2, per, CAP...  3.25 us
    pallas_call x1, Pallas kernels, on_device(): pl.pallas_call(invert_kernel, out_shape=jax.ShapeDtypeStruct((groups * de...  1.83 us
  transfers between devices with their start and end apart: 1, of which 1 were waited for; matrix products, arithmetic and copies ran while one was open for 0% of the time, Pallas kernels for 6%

profile of v6, /device:TPU:1, one launch (start us, length us, event | category | flops | bytes accessed | tf_op | source)
XLA Modules:
  0.0 56.0 jit_solution(17320716850361488192)
XLA Ops:
  0.0 1.8 %shard_map.83 = s32[128,1,1152]{2,1,0:T(1,128)} custom-call(s32[1]{0:T(128)} %bitcast.place_ref, s32[1,1024]{1,0:T(1,128)} %bitcast.12, s32[1,1024]{1,0:T(1,128)} %bitcast.13, s32[1,32]{1,0:T(1,128)} %bitcast.17), custom_call_target="tpu_custom_call" | custom-call | tf_op jit(solution)/shard_map/pallas_call | solution.py:245
  1.8 11.5 %all-to-all-start = ((s32[128,1,1152]{2,1,0:T(1,128)}), s32[128,1,1152]{2,1,0:T(1,128)S(1)}, u32[]{:S(2)}, u32[]{:S(2)}) async-start(s32[128,1,1152]{2,1,0:T(1,128)} %shard_map.83), calls=%async_computation | async-start | bytes 1179648 | tf_op jit(solution)/shard_map/all_to_all | solution.py:283
  13.3 3.3 %shard_map.82 = (bf16[2,4,64,1024]{3,2,1,0:T(8,128)(2,1)S(1)}, bf16[2,4,64,1024]{3,2,1,0:T(8,128)(2,1)S(1)}, bf16[16,64,1024]{2,1,0:T(8,128)(2,1)}, f32[64,128]{1,0:T(8,128)S(1)}, bf16[1056,256]{1,0:T(8,128)(2,1)S(1)}) custom-call(s32[1]{0:T(128)} %bitcast.1.place_ref, bf16[64,32768]{1,0:T(8,128)(2,1)} %dos_hbm.1, s32[1,1024]{1,0:T(1,128)} %bitcast.14, ...), custom_call_target="tpu_custom_call" | custom-call | tf_op jit(solution)/shard_map/pallas_call | solution.py:261
  16.6 11.3 %all-to-all-done.got_ref = s32[128,1,1152]{2,1,0:T(1,128)S(1)} async-done(((s32[128,1,1152]{2,1,0:T(1,128)}), s32[128,1,1152]{2,1,0:T(1,128)S(1)}, u32[]{:S(2)}, u32[]{:S(2)}) %all-to-all-start) | async-done | bytes 589856 | tf_op jit(solution)/shard_map/all_to_all | solution.py:283
  27.9 9.2 %shard_map.84 = bf16[4,32,16,128]{3,2,1,0:T(8,128)(2,1)S(1)} custom-call(s32[1]{0:T(128)} %bitcast.place_ref, bf16[2,4,64,1024]{3,2,1,0:T(8,128)(2,1)S(1)} %get-tuple-element.10.x0, bf16[2,4,64,1024]{3,2,1,0:T(8,128)(2,1)S(1)} %get-tuple-element.11.x1, bf16[16,64,1024]{2,1,0:T(8,128)(2,1)} %get-tuple-element.12.xs_hbm, ...), custom_call_target="tpu_custom_call" | custom-call | tf_op jit(solution)/shard_map/pallas_call | solution.py:284
  37.1 18.0 %all_to_all.10 = bf16[128,16,128]{2,1,0:T(8,128)(2,1)S(1)} all-to-all(bf16[128,16,128]{2,1,0:T(8,128)(2,1)S(1)} %bitcast.11), channel_id=1, replica_groups=mesh['grp'=4,'dev'=32] {'grp','dev'}, dimensions={0} | all-to-all | bytes 1048576 | tf_op jit(solution)/shard_map/all_to_all | solution.py:297
  55.1 1.0 %shard_map.85 = f32[32,256]{1,0:T(8,128)} custom-call(s32[1]{0:T(128)} %bitcast.place_ref, bf16[4,32,16,128]{3,2,1,0:T(8,128)(2,1)S(1)} %bitcast.10, bf16[1056,256]{1,0:T(8,128)(2,1)S(1)} %get-tuple-element.14.proj_ref), custom_call_target="tpu_custom_call" | custom-call | tf_op jit(solution)/shard_map/pallas_call | solution.py:298
Async XLA Ops:
  1.8 26.0 %all-to-all-start = ((s32[128,1,1152]{2,1,0:T(1,128)}), s32[128,1,1152]{2,1,0:T(1,128)S(1)}, u32[]{:S(2)}, u32[]{:S(2)}) async-start(s32[128,1,1152]{2,1,0:T(1,128)} %shard_map.83), calls=%async_computation | async-start | bytes 1179648 | tf_op jit(solution)/shard_map/all_to_all | solution.py:283

commit v7 on v6

--- a/solution.py
+++ b/solution.py
@@ -14,7 +14,7 @@
 HIGH = SECTION // LOW
 CAP = 64
 LANES = 128
-UNROLL1, UNROLL2, UNROLL3, UNROLL4, FUSED = 16, 64, 32, 8, 4
+UNROLL1, UNROLL2, UNROLL3, UNROLL4, FUSED = 16, 64, 32, 8, 8
 BF = jnp.bfloat16
 F32 = jnp.float32
 NT = (((1,), (1,)), ((), ()))

time: 56.3 us -> 56.3 us (level)
  no operation moved by 1% of the time
where the time goes in v7:
time: 56.3 us; the launch traced here: 56 us
  blocking collectives  18 us (32%)
  Pallas kernels  15.3 us (27%)
  starting transfers between devices  11.5 us (20%)
  waiting for transfers between devices  11.3 us (20%)
    all_to_all x1, blocking collectives, on_device(): lax.all_to_all(mixed, both, 0, 0, tiled=True).reshape(groups, devs, 16, 128)  18 us
    all_to_all x1, starting transfers between devices, on_device(): got = lax.all_to_all(send, both, 0, 0, tiled=True)  11.5 us
    all_to_all x1, waiting for transfers between devices, on_device(): got = lax.all_to_all(send, both, 0, 0, tiled=True)  11.3 us
    pallas_call x1, Pallas kernels, on_device(): pl.pallas_call(mix_kernel, out_shape=jax.ShapeDtypeStruct((groups, devs,...  9.21 us
    pallas_call x1, Pallas kernels, on_device(): pl.pallas_call(ready_kernel, out_shape=(jax.ShapeDtypeStruct((2, per, CAP...  3.25 us
    pallas_call x1, Pallas kernels, on_device(): pl.pallas_call(invert_kernel, out_shape=jax.ShapeDtypeStruct((groups * de...  1.83 us
  transfers between devices with their start and end apart: 1, of which 1 were waited for; matrix products, arithmetic and copies ran while one was open for 0% of the time, Pallas kernels for 6%

profile of v7, /device:TPU:1, one launch (start us, length us, event | category | flops | bytes accessed | tf_op | source)
XLA Modules:
  0.0 56.0 jit_solution(16760138402819990980)
XLA Ops:
  0.0 1.8 %shard_map.83 = s32[128,1,1152]{2,1,0:T(1,128)} custom-call(s32[1]{0:T(128)} %bitcast.place_ref, s32[1,1024]{1,0:T(1,128)} %bitcast.12, s32[1,1024]{1,0:T(1,128)} %bitcast.13, s32[1,32]{1,0:T(1,128)} %bitcast.17), custom_call_target="tpu_custom_call" | custom-call | tf_op jit(solution)/shard_map/pallas_call | solution.py:245
  1.8 11.5 %all-to-all-start = ((s32[128,1,1152]{2,1,0:T(1,128)}), s32[128,1,1152]{2,1,0:T(1,128)S(1)}, u32[]{:S(2)}, u32[]{:S(2)}) async-start(s32[128,1,1152]{2,1,0:T(1,128)} %shard_map.83), calls=%async_computation | async-start | bytes 1179648 | tf_op jit(solution)/shard_map/all_to_all | solution.py:283
  13.3 3.3 %shard_map.82 = (bf16[2,4,64,1024]{3,2,1,0:T(8,128)(2,1)S(1)}, bf16[2,4,64,1024]{3,2,1,0:T(8,128)(2,1)S(1)}, bf16[16,64,1024]{2,1,0:T(8,128)(2,1)}, f32[64,128]{1,0:T(8,128)S(1)}, bf16[1056,256]{1,0:T(8,128)(2,1)S(1)}) custom-call(s32[1]{0:T(128)} %bitcast.1.place_ref, bf16[64,32768]{1,0:T(8,128)(2,1)} %dos_hbm.1, s32[1,1024]{1,0:T(1,128)} %bitcast.14, ...), custom_call_target="tpu_custom_call" | custom-call | tf_op jit(solution)/shard_map/pallas_call | solution.py:261
  16.6 11.3 %all-to-all-done.got_ref = s32[128,1,1152]{2,1,0:T(1,128)S(1)} async-done(((s32[128,1,1152]{2,1,0:T(1,128)}), s32[128,1,1152]{2,1,0:T(1,128)S(1)}, u32[]{:S(2)}, u32[]{:S(2)}) %all-to-all-start) | async-done | bytes 589856 | tf_op jit(solution)/shard_map/all_to_all | solution.py:283
  27.9 9.2 %shard_map.84 = bf16[4,32,16,128]{3,2,1,0:T(8,128)(2,1)S(1)} custom-call(s32[1]{0:T(128)} %bitcast.place_ref, bf16[2,4,64,1024]{3,2,1,0:T(8,128)(2,1)S(1)} %get-tuple-element.10.x0, bf16[2,4,64,1024]{3,2,1,0:T(8,128)(2,1)S(1)} %get-tuple-element.11.x1, bf16[16,64,1024]{2,1,0:T(8,128)(2,1)} %get-tuple-element.12.xs_hbm, ...), custom_call_target="tpu_custom_call" | custom-call | tf_op jit(solution)/shard_map/pallas_call | solution.py:284
  37.1 18.0 %all_to_all.10 = bf16[128,16,128]{2,1,0:T(8,128)(2,1)S(1)} all-to-all(bf16[128,16,128]{2,1,0:T(8,128)(2,1)S(1)} %bitcast.11), channel_id=1, replica_groups=mesh['grp'=4,'dev'=32] {'grp','dev'}, dimensions={0} | all-to-all | bytes 1048576 | tf_op jit(solution)/shard_map/all_to_all | solution.py:297
  55.1 1.0 %shard_map.85 = f32[32,256]{1,0:T(8,128)} custom-call(s32[1]{0:T(128)} %bitcast.place_ref, bf16[4,32,16,128]{3,2,1,0:T(8,128)(2,1)S(1)} %bitcast.10, bf16[1056,256]{1,0:T(8,128)(2,1)S(1)} %get-tuple-element.14.proj_ref), custom_call_target="tpu_custom_call" | custom-call | tf_op jit(solution)/shard_map/pallas_call | solution.py:298
Async XLA Ops:
  1.8 26.0 %all-to-all-start = ((s32[128,1,1152]{2,1,0:T(1,128)}), s32[128,1,1152]{2,1,0:T(1,128)S(1)}, u32[]{:S(2)}, u32[]{:S(2)}) async-start(s32[128,1,1152]{2,1,0:T(1,128)} %shard_map.83), calls=%async_computation | async-start | bytes 1179648 | tf_op jit(solution)/shard_map/all_to_all | solution.py:283
